TPU v7x, 32 devices: a whole 2x2x4 slice. The times are simulated.
32 devices in a mesh: pair: 4 (over y, core), fold: 8 (over z, x).
Axes of the slice: x: 2, y: 2, z: 4, core: 2. Of those that a mesh axis runs over, the one named last changes fastest.
Arguments:
- amplitudes: bfloat16 [4, 80, 640, 640], P(None, 'pair', 'fold'), may hold values from -6 to 6
- cycle_block: bfloat16 [640, 80, 8, 640], P('fold', None, 'pair'), may hold values from -0.078125 to 0.078125
- occ_sizes: int32 [8], replicated, may hold values from 1 to 20, 80 in all
- vir_sizes: int32 [8], replicated, may hold values from 1 to 160, 640 in all
- window_i: int32 [4], replicated, may hold values from 0 to 79
- window_occ: int32 [8], replicated, may hold values from 0 to 79
Outputs:
- residual: bfloat16 [4, 640, 8, 640], P(None, 'fold', 'pair')
Inputs may be any that keep to these rules, and one draw needn't show every extreme that they name: `occ_sizes`: the entries sum to 80. `vir_sizes`: the entries sum to 640.
All inputs are finite; a program needn't handle non-finite values.
Results may differ from a plain program's by a relative error of at most 0.001.
Values may be sent and summed in bfloat16 or wider, within the bound.
A program may use at most 128 MiB of HBM per device.

v0:
```python
import functools

import jax
import jax.numpy as jnp
from jax import lax
from jax.experimental import pallas as pl
from jax.experimental.pallas import tpu as pltpu
from jax.sharding import PartitionSpec as P

LANES = 128
EARLY = 2
FOLDS = 4


def irrep_labels(sizes, count):
    boundaries = jnp.cumsum(sizes)
    positions = jnp.arange(count, dtype=jnp.int32)
    return jnp.sum((positions[:, None] >= boundaries[None, :]).astype(jnp.int32), axis=1)


def label_lookup(orbitals, labels, count):
    matches = orbitals[:, None] == jnp.arange(count, dtype=jnp.int32)[None, :]
    return jnp.sum(jnp.where(matches, labels[None, :], 0), axis=1)


def multiply_kernel(lhs_ref, *refs):
    rhs_refs, (row_ref, col_ref, out_ref) = refs[:FOLDS], refs[FOLDS:]
    n_pair = lhs_ref.shape[0]
    j_local = rhs_refs[0].shape[0]
    rows = row_ref[0].astype(jnp.bfloat16)
    left = jnp.concatenate([lhs_ref[p, 0] for p in range(n_pair)], axis=0)
    totals = [None] * j_local
    for s in range(FOLDS):
        keep = rows == col_ref[s].astype(jnp.bfloat16)
        part = jnp.where(keep, left, jnp.zeros_like(left))
        for j in range(j_local):
            term = jnp.dot(part, rhs_refs[s][j], preferred_element_type=jnp.float32)
            totals[j] = term if s == 0 else totals[j] + term
    for j, total in enumerate(totals):
        count, width = total.shape
        rest = width - LANES
        step = count * rest // LANES
        base = j * (count + step)
        out_ref[0, base:base + count] = total[:, :LANES]
        out_ref[0, base + count:base + count + step] = jnp.concatenate(
            [total[t * step:(t + 1) * step, LANES:] for t in range(LANES // rest)], axis=1
        )


def multiply(gathered, packed_w, row_labels, col_labels):
    n_pair, n_fold, span, depth = gathered.shape
    j_local, _, width = packed_w[0].shape
    rows = n_pair * span
    lines = j_local * rows * width // LANES
    rhs_spec = pl.BlockSpec(packed_w[0].shape, lambda f: (0, 0, 0), pipeline_mode=pl.Buffered(1))
    return pl.pallas_call(
        multiply_kernel,
        grid=(n_fold,),
        out_shape=jax.ShapeDtypeStruct((n_fold, lines, LANES), jnp.float32),
        in_specs=[pl.BlockSpec((n_pair, 1, span, depth), lambda f: (0, f, 0, 0))]
        + [rhs_spec] * FOLDS
        + [
            pl.BlockSpec((1, rows, 1), lambda f: (f, 0, 0)),
            pl.BlockSpec(col_labels.shape, lambda f: (0, 0, 0)),
        ],
        out_specs=pl.BlockSpec((1, lines, LANES), lambda f: (f, 0, 0)),
        compiler_params=pltpu.CompilerParams(vmem_limit_bytes=48 << 20),
        cost_estimate=pl.CostEstimate(
            flops=2 * n_fold * rows * FOLDS * depth * j_local * width,
            bytes_accessed=2 * gathered.size + 2 * FOLDS * packed_w[0].size,
            transcendentals=0,
        ),
    )(gathered, *packed_w, row_labels, col_labels)


def refold_kernel(occ_ref, moved_ref, row_ref, vir_ref, out_ref, wide_ref):
    n_pair, n_i, k_local, a_sub, v_pack = moved_ref.shape
    here, _, depth = out_ref.shape
    c_local = v_pack // here
    k_pack = depth // c_local
    for i in range(n_i):
        labels = row_ref[i] ^ vir_ref[0]
        for kappa in range(k_pack):
            total = jnp.zeros((a_sub, v_pack), jnp.float32)
            for s in range(FOLDS):
                k = s * k_pack + kappa
                piece = moved_ref[k // k_local, i, k % k_local].astype(jnp.float32)
                total = jnp.where(labels == occ_ref[k], piece, total)
            for f in range(here):
                wide_ref[f, i * a_sub:(i + 1) * a_sub, kappa * c_local:(kappa + 1) * c_local] = (
                    total[:, f * c_local:(f + 1) * c_local]
                )
    out_ref[...] = wide_ref[...].astype(out_ref.dtype)


def refold(moved, row_labels, vir_labels, occ_labels, c_local):
    _, n_i, _, a_sub, v_pack = moved.shape
    here = v_pack // c_local
    shape = (FOLDS * here, n_i * a_sub, occ_labels.shape[0] // FOLDS * c_local)
    return pl.pallas_call(
        refold_kernel,
        grid=(FOLDS,),
        out_shape=jax.ShapeDtypeStruct(shape, moved.dtype),
        in_specs=[
            pl.BlockSpec(memory_space=pltpu.SMEM),
            pl.BlockSpec(moved.shape, lambda q: (0, 0, 0, 0, 0), pipeline_mode=pl.Buffered(1)),
            pl.BlockSpec((n_i, a_sub, 1), lambda q: (0, 0, 0)),
            pl.BlockSpec((1, 1, v_pack), lambda q: (q, 0, 0)),
        ],
        out_specs=pl.BlockSpec((here,) + shape[1:], lambda q: (q, 0, 0)),
        scratch_shapes=[pltpu.VMEM((here,) + shape[1:], jnp.float32)],
        compiler_params=pltpu.CompilerParams(vmem_limit_bytes=40 << 20),
    )(occ_labels, moved, row_labels[..., None], vir_labels.reshape(FOLDS, 1, v_pack))


def body(n_pair, n_fold, amplitudes, cycle_block, occ_sizes, vir_sizes, window_i, window_occ):
    c_local, occ_total, j_local, vir_total = cycle_block.shape
    n_i, k_local, a_rows, _ = amplitudes.shape
    v_pack = vir_total // FOLDS
    k_pack = occ_total // FOLDS
    a_sub = a_rows // n_pair
    fold = lax.axis_index("fold")
    pair = lax.axis_index("pair")
    occ_labels = irrep_labels(occ_sizes, occ_total)
    vir_labels = irrep_labels(vir_sizes, vir_total)
    c_labels = lax.dynamic_slice_in_dim(vir_labels, fold * c_local, c_local)
    a_labels = lax.dynamic_slice_in_dim(vir_labels, fold * a_rows, a_rows)
    k_labels = lax.dynamic_slice_in_dim(occ_labels, pair * k_local, k_local)
    i_labels = label_lookup(window_i, occ_labels, occ_total)
    j_orbitals = lax.dynamic_slice_in_dim(window_occ, pair * j_local, j_local)
    j_labels = label_lookup(j_orbitals, occ_labels, occ_total)

    ika = i_labels[:, None, None] ^ k_labels[None, :, None] ^ a_labels[None, None, :]
    packed_c = 0
    for q in range(FOLDS):
        cut = slice(q * v_pack, (q + 1) * v_pack)
        keep = ika[..., None] == vir_labels[cut]
        packed_c = packed_c + jnp.where(keep, amplitudes[..., cut], 0)
    parts = packed_c.reshape(n_i, k_local, n_pair, a_sub, v_pack).transpose(2, 0, 1, 3, 4)
    moved = lax.all_to_all(parts, "pair", split_axis=0, concat_axis=0, tiled=True)
    depth = k_pack * c_local
    def pack_slices(source, wanted):
        made = []
        for s in wanted:
            block = source[:, s * k_pack:(s + 1) * k_pack].transpose(2, 1, 0, 3)
            own_k = occ_labels[s * k_pack:(s + 1) * k_pack]
            jkc = j_labels[:, None, None] ^ own_k[None, :, None] ^ c_labels[None, None, :]
            folded = 0
            for q in range(FOLDS):
                cut = slice(q * v_pack, (q + 1) * v_pack)
                keep = jkc[..., None] == vir_labels[cut]
                folded = folded + jnp.where(keep, block[..., cut], 0)
            made.append(folded.reshape(j_local, depth, v_pack))
        return made

    early = pack_slices(cycle_block, range(EARLY))
    moved, *early = lax.optimization_barrier((moved, *early))
    own_a = lax.dynamic_slice_in_dim(a_labels, pair * a_sub, a_sub)
    packed_k = refold(moved, i_labels[:, None] ^ own_a[None, :], vir_labels, occ_labels, c_local)
    packed_k, source = lax.optimization_barrier((packed_k, cycle_block))
    packed_w = list(early) + pack_slices(source, range(EARLY, FOLDS))
    relaid = lax.all_to_all(packed_k, "fold", split_axis=0, concat_axis=0, tiled=True)
    gathered = lax.all_gather(relaid, "pair", axis=0, tiled=False)

    row_a = vir_labels.reshape(n_fold, n_pair, a_sub)
    row_labels = (row_a[:, :, None, :] ^ i_labels[:, None]).reshape(n_fold, -1, 1)
    col_labels = (occ_labels[:, None] ^ c_labels[None, :]).reshape(FOLDS, 1, depth)
    count = n_pair * n_i * a_sub
    rest = v_pack - LANES
    step = count * rest // LANES
    partial_sum = multiply(gathered, packed_w, row_labels, col_labels)
    summed = lax.psum_scatter(
        partial_sum.reshape(-1, LANES), "fold", scatter_dimension=0, tiled=True
    ).astype(jnp.bfloat16)
    columns = []
    for j in range(j_local):
        own = summed[j * (count + step):(j + 1) * (count + step)]
        tail = jnp.concatenate(
            [own[count:, t * rest:(t + 1) * rest] for t in range(LANES // rest)], axis=0
        )
        columns.append(jnp.concatenate([own[:count], tail], axis=1))
    own = jnp.stack(columns, axis=1).reshape(n_pair, n_i, a_sub, j_local, v_pack)
    own = own.transpose(1, 0, 2, 3, 4).reshape(n_i, a_rows, j_local, v_pack)
    iaj = i_labels[:, None, None] ^ a_labels[None, :, None] ^ j_labels[None, None, :]
    keep = iaj[..., None] == vir_labels
    return jnp.where(keep, jnp.concatenate([own] * FOLDS, axis=-1), 0)


def solution(mesh):
    sizes = mesh.shape["pair"], mesh.shape["fold"]
    placed = (P(None, "pair", "fold", None), P("fold", None, "pair", None), P(), P(), P(), P())

    def run(*args):
        return body(*sizes, *args)

    return jax.shard_map(
        run, mesh=mesh, in_specs=placed, out_specs=P(None, "fold", "pair", None), check_vma=False
    )
```

profile of v0, /device:TPU:17, one launch (start us, length us, event | category | flops | bytes accessed | tf_op | source)
XLA Modules:
  0.0 305.5 jit_solution(14205314819769236511)
XLA Ops:
  6.5 0.8 reduce-window.16
  7.4 0.1 convert_reduce_fusion.1.occ_ref
  7.5 0.8 reduce-window.17
  8.3 0.1 convert_reduce_fusion
  8.6 0.8 select_reduce_fusion
  9.5 0.1 broadcast_xor_fusion.7
  9.6 9.5 %fusion.2 = bf16[4,20,80,160]{3,2,1,0:T(8,128)(2,1)S(1)} fusion(bf16[4,20,80,640]{3,2,1,0:T(8,128)(2,1)} %param.6, s32[160]{0:T(256)S(1)} %get-tuple-element.34, s32[160]{0:T(256)S(1)} %get-tuple-element.35, s32[160]{0:T(256)S(1)} %get-tuple-element.36, s32[160]{0:T(256)S(1)} %get-tuple-element.33, s32[4,20,80]{2,1,0:T(8,128)S(1)} %broadcast_xor_fusion.7), kind=kLoop, calls=%fused_computation.26 | loop fusion | flops 11264000 | bytes 10268160 | tf_op jit(solution)/shard_map/add | solution.py:138
  19.1 2.5 copy.69
  21.7 2.9 copy.70
  24.6 5.4 %all-to-all-start = ((bf16[4,4,20,20,160]{4,1,3,2,0:T(4,128)(2,1)}), bf16[4,4,20,20,160]{4,1,3,2,0:T(4,128)(2,1)}, u32[]{:S(2)}, u32[]{:S(2)}) async-start(bf16[4,4,20,20,160]{4,1,3,2,0:T(4,128)(2,1)} %copy.70), calls=%async_computation | async-start | bytes 6553600 | tf_op jit(solution)/shard_map/all_to_all | solution.py:140
  30.1 0.2 fusion.15
  30.3 7.1 %slice_bitcast_fusion.2 = (bf16[2,20,80,640]{3,0,1,2:T(2,128)(2,1)S(1)}, bf16[2,20,80,640]{3,0,1,2:T(2,128)(2,1)S(1)}) fusion(bf16[80,80,2,640]{3,2,1,0:T(2,128)(2,1)} %param.7), kind=kLoop, calls=%fused_computation.22 | loop fusion | bytes 16384000 | tf_op jit(solution)/shard_map/transpose | solution.py:145
  37.4 0.1 broadcast_xor_fusion.9
  37.5 1.6 broadcast_xor_fusion.1
  39.1 28.3 %fusion.8 = (bf16[2,20,80,160]{3,0,1,2:T(2,128)(2,1)S(1)}, bf16[2,20,80,160]{3,0,1,2:T(2,128)(2,1)}) fusion(bf16[2,20,80,640]{3,0,1,2:T(2,128)(2,1)S(1)} %get-tuple-element.17, s32[2,20,80]{0,1,2:T(8,128)S(1)} %get-tuple-element.38, s32[160]{0:T(256)S(1)} %get-tuple-element.34, s32[160]{0:T(256)S(1)} %get-tuple-element.35, s32[160]{0:T(256)S(1)} %get-tuple-element.36, ...), kind=kLoop, calls=%fused_computation.33 | loop fusion | flops 11264000 | bytes 10268160 | tf_op jit(solution)/shard_map/add | solution.py:152
  67.5 0.1 reshape.401.vir_ref
  67.5 0.3 copy.72
  67.9 1.1 copy-done.1
  69.0 0.3 copy.71
  69.3 0.1 dynamic_slice.19
  69.5 2.6 copy.73.moved_ref
  72.1 6.2 %shard_map.64 = bf16[8,80,1600]{2,1,0:T(8,128)(2,1)S(1)} custom-call(s32[80]{0:T(128)S(1)} %convert_reduce_fusion.1.occ_ref, bf16[4,4,20,20,160]{4,3,2,1,0:T(8,128)(2,1)S(1)} %copy.73.moved_ref, s32[4,20,1]{2,1,0:T(8,128)S(1)} %broadcast_xor_fusion.6.row_ref, s32[4,1,160]{2,1,0:T(1,128)S(1)} %reshape.401.vir_ref), custom_call_target="tpu_custom_call" | custom-call | tf_op jit(solution)/shard_map/pallas_call | solution.py:100
  78.3 53.2 %all_to_all.10 = bf16[8,80,1600]{2,1,0:T(8,128)(2,1)} all-to-all(bf16[8,80,1600]{2,1,0:T(8,128)(2,1)S(1)} %shard_map.64), channel_id=1, replica_groups=mesh['pair'=4,'fold'=8] {'fold'}, dimensions={0} | all-to-all | bytes 4096000 | tf_op jit(solution)/shard_map/all_to_all | solution.py:162
  131.5 0.2 reduce-scatter.4.cloned.1.call-start
  131.8 0.1 xor.314
  131.8 0.1 xor.307
  132.1 0.1 xor.322
  132.3 0.1 xor.311
  132.4 1.5 xor.321
  134.0 2.6 broadcast_xor_fusion.refs_4_
  136.6 7.2 %slice_bitcast_fusion = (bf16[2,20,80,640]{3,0,1,2:T(2,128)(2,1)S(1)}, bf16[2,20,80,640]{3,0,1,2:T(2,128)(2,1)S(1)}) fusion(bf16[80,80,2,640]{3,2,1,0:T(2,128)(2,1)} %param.7), kind=kLoop, calls=%fused_computation.20 | loop fusion | bytes 16384000 | tf_op jit(solution)/shard_map/transpose | solution.py:145
  143.9 27.8 %fusion.14 = (bf16[2,20,80,160]{3,0,1,2:T(2,128)(2,1)S(1)}, bf16[2,20,80,160]{3,0,1,2:T(2,128)(2,1)S(1)}) fusion(bf16[2,20,80,640]{3,0,1,2:T(2,128)(2,1)S(1)} %get-tuple-element.15, s32[2,20,80]{0,1,2:T(8,128)S(1)} %copy-done.2, s32[160]{0:T(256)S(1)} %get-tuple-element.34, s32[160]{0:T(256)S(1)} %get-tuple-element.35, s32[160]{0:T(256)S(1)} %get-tuple-element.36, ...), kind=kLoop, calls=%fused_computation.39 | loop fusion | flops 11264000 | bytes 10268160 | tf_op jit(solution)/shard_map/add | solution.py:152
  171.6 1.6 copy.74
  173.2 1.5 copy.75
  174.7 16.8 %all-gather.3.cloned.1.call-done = bf16[32,80,1600]{2,1,0:T(8,128)(2,1)} async-done(((bf16[8,80,1600]{2,1,0:T(8,128)(2,1)}), bf16[32,80,1600]{2,1,0:T(8,128)(2,1)}) %all-gather.3.cloned.1.call-update) | async-done | bytes 8192016 | tf_op jit(solution)/shard_map/all_gather | solution.py:163
  191.5 1.3 copy-done
  192.8 24.5 %shard_map.65 = f32[8,800,128]{2,1,0:T(8,128)} custom-call(bf16[4,8,80,1600]{3,2,1,0:T(8,128)(2,1)} %bitcast.33, bf16[2,1600,160]{2,1,0:T(8,128)(2,1)S(1)} %bitcast.26, bf16[2,1600,160]{2,1,0:T(8,128)(2,1)S(1)} %bitcast.25, bf16[2,1600,160]{2,1,0:T(8,128)(2,1)} %bitcast.29, bf16[2,1600,160]{2,1,0:T(8,128)(2,1)} %bitcast.30, s32[8,320,1]{2,1,0:T(8,128)S(1)} %copy-done, ...), custom_call_target="tpu_custom_call" | custom-call | flops 10485760000 | bytes 12288000 | tf_op jit(solution)/shard_map/pallas_call | solution.py:56
  217.4 0.1 broadcast_xor_fusion.5
  217.5 74.5 %reduce-scatter.4.cloned.1.call-done = f32[800,128]{1,0:T(8,128)} async-done(((f32[6400,128]{1,0:T(8,128)}), f32[800,128]{1,0:T(8,128)}) %reduce-scatter.4.cloned.1.call-update) | async-done | bytes 409616
  292.0 1.2 copy.85
  293.1 0.1 fusion.16
  293.2 0.1 fusion.17
  293.3 0.1 maximum_maximum_fusion
  293.4 0.1 copy.82
  293.6 0.1 copy.81
  293.8 0.1 maximum_bitcast_fusion
  293.9 0.3 copy.83
  294.2 4.5 %compare_select_fusion.20 = bf16[4,80,2,640]{3,2,1,0:T(2,128)(2,1)} fusion(bf16[4,80,2,160]{3,2,1,0:T(2,128)(2,1)S(1)} %bitcast.31, s32[640]{0:T(1024)S(1)} %convert_reduce_fusion, s32[4,80,2]{2,1,0:T(8,128)S(1)} %broadcast_xor_fusion.5), kind=kLoop, calls=%fused_computation.27 | loop fusion | flops 4096000 | bytes 1029120 | tf_op jit(solution)/shard_map/jit(_where)/select_n | solution.py:186
  (27 shorter events, 0.9 us)
Async XLA Ops:
  24.6 5.5 %copy-start.4 = (s32[8]{0:T(128)S(1)}, s32[8]{0:T(128)}, u32[]{:S(2)}) copy-start(s32[8]{0:T(128)} %param.11) | copy-start | bytes 100
  24.6 44.9 %all-to-all-start = ((bf16[4,4,20,20,160]{4,1,3,2,0:T(4,128)(2,1)}), bf16[4,4,20,20,160]{4,1,3,2,0:T(4,128)(2,1)}, u32[]{:S(2)}, u32[]{:S(2)}) async-start(bf16[4,4,20,20,160]{4,1,3,2,0:T(4,128)(2,1)} %copy.70), calls=%async_computation | async-start | bytes 6553600 | tf_op jit(solution)/shard_map/all_to_all | solution.py:140
  30.0 161.5 %all-gather.3.cloned.1.call-start = ((), (), s32[]{:S(2)}) async-start(), calls=%async_computation.3 | async-start | bytes 10649600 | tf_op jit(solution)/shard_map/all_gather | solution.py:163
  67.5 1.4 copy-start.1
  131.5 160.4 %reduce-scatter.4.cloned.1.call-start = ((), (), s32[]{:S(2)}) async-start(), calls=%async_computation.4 | async-start | bytes 3686400
  136.6 7.3 %copy-start.2 = (s32[2,20,80]{0,1,2:T(8,128)S(1)}, s32[2,20,80]{0,1,2:T(8,128)}, u32[]{:S(2)}) copy-start(s32[2,20,80]{0,1,2:T(8,128)} %get-tuple-element.37) | copy-start | bytes 38404
  136.6 7.3 %copy-start.3 = (s32[2,20,80]{0,1,2:T(8,128)S(1)}, s32[2,20,80]{0,1,2:T(8,128)}, u32[]{:S(2)}) copy-start(s32[2,20,80]{0,1,2:T(8,128)} %get-tuple-element.39) | copy-start | bytes 38404
  191.5 1.3 copy-start
Sparse Core Ops, SparseCore 0:
  131.6 59.8 all-gather.2
  217.4 74.4 reduce-scatter.3
where the time goes:
time: 309 us; the launch traced here: 306 us
  waiting for transfers between devices  91.3 us (30%)
  other arithmetic  77.9 us (25%)
  blocking collectives  53.2 us (17%)
  local copies, waits for them, and re-layouts  33.1 us (11%)
  Pallas kernels  30.7 us (10%)
  between operations  13.6 us (4%)
  starting transfers between devices  5.67 us (2%)
    unnamed x3, waiting for transfers between devices  74.5 us
    add x2, other arithmetic, pack_slices(): folded = folded + jnp.where(keep, block[..., cut], 0)  56.1 us
    all_to_all x1, blocking collectives, body(): lax.all_to_all(packed_k, 'fold', split_axis=0, concat_axis=0, tiled=True)  53.2 us
    pallas_call x1, Pallas kernels, multiply(): pl.pallas_call(multiply_kernel, grid=(n_fold,), out_shape=jax.ShapeDtypeS...  24.5 us
    all_gather x1, waiting for transfers between devices, body(): gathered = lax.all_gather(relaid, 'pair', axis=0, tiled=False)  16.8 us
    transpose x2, local copies, waits for them, and re-layouts, pack_slices(): block = source[:, s * k_pack:(s + 1) * k_pack].transpose(2, 1, 0, 3)  14.3 us
    add x1, other arithmetic, body(): packed_c = packed_c + jnp.where(keep, amplitudes[..., cut], 0)  9.53 us
    pallas_call x1, Pallas kernels, refold(): pl.pallas_call(refold_kernel, grid=(FOLDS,), out_shape=jax.ShapeDtypeStru...  6.19 us
  transfers between devices with their start and end apart: 3, of which 2 were waited for; matrix products, arithmetic and copies ran while one was open for 27% of the time, Pallas kernels for 0%

commit v1 on v0

v1 whole, which is shorter than its diff:
```python
import functools

import jax
import jax.numpy as jnp
from jax import lax
from jax.experimental import pallas as pl
from jax.experimental.pallas import tpu as pltpu
from jax.sharding import PartitionSpec as P

LANES = 128
FOLDS = 4
STEPS = 32000.0
FINE = 8.0


def irrep_labels(sizes, count):
    boundaries = jnp.cumsum(sizes)
    positions = jnp.arange(count, dtype=jnp.int32)
    return jnp.sum((positions[:, None] >= boundaries[None, :]).astype(jnp.int32), axis=1)


def label_lookup(orbitals, labels, count):
    matches = orbitals[:, None] == jnp.arange(count, dtype=jnp.int32)[None, :]
    return jnp.sum(jnp.where(matches, labels[None, :], 0), axis=1)


def narrow(labels):
    return labels.astype(jnp.float32).astype(jnp.bfloat16)


def fold_columns(values, rows, lanes):
    v_pack = values.shape[1] // FOLDS
    total = jnp.zeros((values.shape[0], v_pack), values.dtype)
    for q in range(FOLDS):
        cut = slice(q * v_pack, (q + 1) * v_pack)
        total = jnp.where(rows == lanes[:, cut], values[:, cut], total)
    return total


def pack_t_kernel(label_ref, row_ref, vir_ref, t_ref, out_ref):
    piece = pl.program_id(0)
    k_local = t_ref.shape[1]
    rest = t_ref.shape[-1] // FOLDS - LANES
    group = LANES // rest
    tails = []
    for k in range(k_local):
        lanes = narrow(vir_ref[...] ^ label_ref[piece * k_local + k])
        total = fold_columns(t_ref[0, k, 0], row_ref[0], lanes)
        out_ref[0, k] = total[:, :LANES]
        tails.append(total[:, LANES:])
        if k == k_local - 1:
            tails += [jnp.zeros_like(tails[0])] * (group - len(tails))
        if len(tails) == group:
            out_ref[0, k_local + k // group] = jnp.concatenate(tails, axis=1)
            tails = []


def pack_t(amplitudes, ik_labels, a_labels, vir_labels, n_pair):
    n_i, k_local, a_rows, vir_total = amplitudes.shape
    split = n_pair // n_i
    rows = a_rows // split
    rest = vir_total // FOLDS - LANES
    depth = k_local + -(-k_local * rest // LANES)
    source = amplitudes.reshape(n_i, k_local, split, rows, vir_total)
    labels = jnp.broadcast_to(ik_labels[:, None, :], (n_i, split, k_local)).reshape(-1)
    return pl.pallas_call(
        pack_t_kernel,
        grid=(n_pair,),
        out_shape=jax.ShapeDtypeStruct((n_pair, depth, rows, LANES), amplitudes.dtype),
        in_specs=[
            pl.BlockSpec(memory_space=pltpu.SMEM),
            pl.BlockSpec((1, rows, 1), lambda p: (p % split, 0, 0)),
            pl.BlockSpec((1, vir_total), lambda p: (0, 0)),
            pl.BlockSpec((1, k_local, 1, rows, vir_total), lambda p: (p // split, 0, p % split, 0, 0)),
        ],
        out_specs=pl.BlockSpec((1, depth, rows, LANES), lambda p: (p, 0, 0, 0)),
        compiler_params=pltpu.CompilerParams(vmem_limit_bytes=32 << 20),
    )(labels, narrow(a_labels).reshape(split, rows, 1), vir_labels[None, :], source)


def pack_w_kernel(occ_ref, row_ref, vir_ref, w_ref, out_ref, main_ref, rest_ref):
    block = pl.program_id(0)
    c_local, ks, j_local, vir_total = w_ref.shape
    rest = vir_total // FOLDS - LANES
    for k in range(ks):
        lanes = narrow(vir_ref[...] ^ occ_ref[block * ks + k])
        values = w_ref[:, k].reshape(c_local * j_local, vir_total)
        total = fold_columns(values, row_ref[...], lanes).astype(jnp.float32)
        main_ref[...] = total[:, :LANES]
        rest_ref[:, :rest] = total[:, LANES:]
        for j in range(j_local):
            own = pl.ds(j, c_local, stride=j_local)
            out_ref[j, k * c_local:(k + 1) * c_local, :LANES] = main_ref[own, :].astype(out_ref.dtype)
            out_ref[j, k * c_local:(k + 1) * c_local, LANES:] = rest_ref[own, :][:, :rest].astype(out_ref.dtype)


def pack_w(cycle_block, occ_labels, cj_labels, vir_labels):
    c_local, occ_total, j_local, vir_total = cycle_block.shape
    v_pack = vir_total // FOLDS
    ks = 8
    return pl.pallas_call(
        pack_w_kernel,
        grid=(occ_total // ks,),
        out_shape=jax.ShapeDtypeStruct((j_local, occ_total * c_local, v_pack), cycle_block.dtype),
        in_specs=[
            pl.BlockSpec(memory_space=pltpu.SMEM),
            pl.BlockSpec((c_local * j_local, 1), lambda k: (0, 0)),
            pl.BlockSpec((1, vir_total), lambda k: (0, 0)),
            pl.BlockSpec((c_local, ks, j_local, vir_total), lambda k: (0, k, 0, 0)),
        ],
        out_specs=pl.BlockSpec((j_local, ks * c_local, v_pack), lambda k: (0, k, 0)),
        scratch_shapes=[pltpu.VMEM((c_local * j_local, LANES), jnp.float32)] * 2,
        compiler_params=pltpu.CompilerParams(vmem_limit_bytes=32 << 20),
        cost_estimate=pl.CostEstimate(
            flops=0, bytes_accessed=4 * cycle_block.size, transcendentals=0
        ),
    )(occ_labels, narrow(cj_labels).reshape(-1, 1), vir_labels[None, :], cycle_block)


def flip(index, bits, count):
    total, bit = 0, 1
    while bit < count:
        total = total + (index // bit + bits // bit) % 2 * bit
        bit *= 2
    return total


def encode(parts, out_ref):
    top = functools.reduce(jnp.maximum, [jnp.max(jnp.abs(part), axis=1, keepdims=True) for part in parts])
    code = jnp.ceil(jnp.log2(jnp.maximum(top, 1e-30)) * FINE)
    factor = STEPS * jnp.exp2(code * (-1.0 / FINE))
    scaled = [jnp.round(part * factor).astype(jnp.int32) for part in parts]
    rest = [part[:, LANES:] for part in scaled]
    spare = LANES - sum(part.shape[1] for part in rest)
    rest.append(jnp.broadcast_to(code.astype(jnp.int32), (code.shape[0], spare)))
    for j, part in enumerate(scaled):
        out_ref[:, j * LANES:(j + 1) * LANES] = part[:, :LANES].astype(jnp.int16)
    out_ref[:, len(parts) * LANES:] = jnp.concatenate(rest, axis=1).astype(jnp.int16)


def decode(packed, count, width):
    values = packed.astype(jnp.int32).astype(jnp.float32)
    code = values[:, -1:]
    values = values * (jnp.exp2(code * (1.0 / FINE)) / STEPS)
    rest = width - LANES
    return [
        jnp.concatenate(
            [
                values[:, j * LANES:(j + 1) * LANES],
                values[:, count * LANES + j * rest:count * LANES + (j + 1) * rest],
            ],
            axis=1,
        )
        for j in range(count)
    ]


def contract_kernel(
    n_pair, n_fold, occ_ref, own_ref, vir_ref, row_ref, col_ref, moved_ref, w_ref, out_ref,
    wide, held, total, x_out, x_in, z_out, z_in,
    copy_sem, f_send, f_recv, y_send, y_recv, c_send, c_recv, x_send, x_recv, z_send, z_recv,
):
    pair, fold = lax.axis_index("pair"), lax.axis_index("fold")
    n_y, n_outer, here = n_pair // 2, n_fold // 2, n_fold // FOLDS
    y, core = pair // 2, pair % 2
    outer, half = fold // 2, fold % 2
    mate = y * 2 + 1 - core
    rows, v_pack = own_ref.shape[0], vir_ref.shape[2]
    k_local = moved_ref.shape[1] - -(-moved_ref.shape[1] * (v_pack - LANES) // v_pack)
    k_pack = occ_ref.shape[0] // FOLDS
    c_local = v_pack // here
    depth = k_pack * c_local
    rest = v_pack - LANES
    group = LANES // rest
    j_local = w_ref.shape[0]

    barrier = pltpu.get_barrier_semaphore()
    for step in range(1, n_fold):
        pl.semaphore_signal(barrier, device_id={"fold": (fold + step) % n_fold})
    for step in range(1, n_y):
        pl.semaphore_signal(barrier, device_id={"pair": (y + step) % n_y * 2 + core})
    pl.semaphore_signal(barrier, device_id={"pair": mate})
    pl.semaphore_wait(barrier, n_fold + n_y - 1)

    def to_fold(target):
        return pltpu.make_async_remote_copy(
            src_ref=wide.at[target], dst_ref=held.at[fold, pair],
            send_sem=f_send.at[target], recv_sem=f_recv.at[fold], device_id={"fold": target},
        )

    def from_fold(source):
        return pltpu.make_async_remote_copy(
            src_ref=wide.at[source], dst_ref=held.at[source, pair],
            send_sem=f_send.at[source], recv_sem=f_recv.at[source], device_id={"fold": source},
        )

    def over_y(source, step):
        other = (y + step) % n_y
        return pltpu.make_async_remote_copy(
            src_ref=held.at[source, pair], dst_ref=held.at[source, pair],
            send_sem=y_send.at[source, other], recv_sem=y_recv.at[source, y],
            device_id={"pair": other * 2 + core},
        )

    def from_y(source, step):
        other = (y + step) % n_y
        slot = held.at[source, other * 2 + core]
        return pltpu.make_async_remote_copy(
            src_ref=slot, dst_ref=slot,
            send_sem=y_send.at[source, other], recv_sem=y_recv.at[source, other],
            device_id={"pair": other * 2 + core},
        )

    def over_core(source, step):
        other = (y + step) % n_y
        slot = held.at[source, other * 2 + core]
        return pltpu.make_async_remote_copy(
            src_ref=slot, dst_ref=slot,
            send_sem=c_send.at[source, other], recv_sem=c_recv.at[source, other],
            device_id={"pair": mate},
        )

    def from_core(source, step):
        other = (y + step) % n_y
        slot = held.at[source, other * 2 + 1 - core]
        return pltpu.make_async_remote_copy(
            src_ref=slot, dst_ref=slot,
            send_sem=c_send.at[source, other], recv_sem=c_recv.at[source, other],
            device_id={"pair": mate},
        )

    def over_x(block):
        return pltpu.make_async_remote_copy(
            src_ref=x_out.at[block], dst_ref=x_in.at[block],
            send_sem=x_send.at[block], recv_sem=x_recv.at[block],
            device_id={"fold": outer * 2 + 1 - half},
        )

    def over_z(block, slot):
        return pltpu.make_async_remote_copy(
            src_ref=z_out.at[block], dst_ref=z_in.at[slot],
            send_sem=z_send.at[block], recv_sem=z_recv.at[slot],
            device_id={"fold": block * 2 + half},
        )

    def own_copy():
        return pltpu.make_async_copy(wide.at[fold], held.at[fold, pair], copy_sem)

    def quarter(step, carry):
        q = flip(fold // here, step, FOLDS)
        labels = narrow(own_ref[...] ^ vir_ref[q])
        pieces = [[] for _ in range(here)]
        for kappa in range(k_pack):
            chosen = jnp.zeros((rows, v_pack), moved_ref.dtype)
            for s in range(FOLDS):
                k = s * k_pack + kappa
                side, inner = k // k_local, k % k_local
                tail = inner % group * rest
                piece = jnp.concatenate(
                    [
                        moved_ref[side, inner],
                        moved_ref[side, k_local + inner // group][:, tail:tail + rest],
                    ],
                    axis=1,
                )
                chosen = jnp.where(labels == occ_ref[k], piece, chosen)
            for f in range(here):
                pieces[f].append(chosen[:, f * c_local:(f + 1) * c_local])
        for f in range(here):
            spare = wide.shape[2] - depth
            if spare:
                pieces[f].append(jnp.zeros((rows, spare), moved_ref.dtype))
            target = q * here + f
            wide[target] = jnp.concatenate(pieces[f], axis=1)
        for f in range(here):
            target = q * here + f

            @pl.when(step * here + f > 0)
            def _():
                other = q * here + (fold + f) % here
                to_fold(other).start()

        return carry

    lax.fori_loop(0, FOLDS, quarter, 0)
    own_copy().start()
    own_copy().wait()

    def source_of(step):
        return flip(outer, step // 2, n_outer) * 2 + (half + 1 + step) % 2

    def relay(source):
        for step in range(1, n_y):
            over_y(source, step).start()
        over_core(source, 0).start()

    def pass_on(source):
        for step in range(1, n_y):
            from_y(source, step).wait_recv()
            over_core(source, step).start()

    relay(fold)
    first = source_of(0)
    from_fold(first).wait_recv()
    relay(first)
    pass_on(first)

    def contract(step, carry):
        source = source_of(step)

        @pl.when(step + 2 < n_fold)
        def _():
            later = source_of(step + 2)
            from_fold(later).wait_recv()
            relay(later)

        @pl.when(step + 1 < n_fold)
        def _():
            pass_on(source_of(step + 1))

        for other in range(n_y):
            from_core(source, other).wait_recv()
        left = jnp.concatenate([held[source, p][:, :depth] for p in range(n_pair)], axis=0)
        labels = row_ref[source]
        parts = [None] * j_local
        for s in range(FOLDS):
            part = jnp.where(labels == col_ref[s], left, jnp.zeros_like(left))
            for j in range(j_local):
                term = jnp.dot(
                    part, w_ref[j, s * depth:(s + 1) * depth], preferred_element_type=jnp.float32
                )
                parts[j] = term if s == 0 else parts[j] + term
        block = flip(outer, step // 2, n_outer)
        for j in range(j_local):
            total[j] = parts[j]

        @pl.when(step % 2 == 0)
        def _():
            encode([total[j] for j in range(j_local)], x_out.at[block])
            over_x(block).start()

        @pl.when(step % 2 == 1)
        def _():
            over_x(block).wait_recv()
            near = decode(x_in[block], j_local, v_pack)
            near = [total[j] + near[j] for j in range(j_local)]

            @pl.when(step == 1)
            def _():
                for j in range(j_local):
                    out_ref[j] = near[j]

            @pl.when(step > 1)
            def _():
                encode(near, z_out.at[block])
                over_z(block, outer).start()

        return carry

    lax.fori_loop(0, n_fold, contract, 0)

    def finish(step, carry):
        block = flip(outer, step, n_outer)
        over_z(block, block).wait_recv()
        far = decode(z_in[block], j_local, v_pack)
        for j in range(j_local):
            out_ref[j] += far[j]
        return carry

    lax.fori_loop(1, n_outer, finish, 0)

    def drain(source, carry):
        @pl.when(source != fold)
        def _():
            to_fold(source).wait_send()

        for step in range(1, n_y):
            over_y(source, step).wait_send()
        for step in range(n_y):
            over_core(source, step).wait_send()
        return carry

    lax.fori_loop(0, n_fold, drain, 0)

    def drain_sums(block, carry):
        over_x(block).wait_send()

        @pl.when(block != outer)
        def _():
            over_z(block, outer).wait_send()

        return carry

    lax.fori_loop(0, n_outer, drain_sums, 0)


def contract_all(n_pair, n_fold, moved, packed_w, occ_labels, own_labels, vir_labels, row_labels, col_labels):
    _, _, rows, _ = moved.shape
    j_local, _, v_pack = packed_w.shape
    depth = col_labels.shape[-1]
    wide = -(-depth // LANES) * LANES
    n_y, n_outer = n_pair // 2, n_fold // 2
    count = n_pair * rows
    lanes = (j_local + -(-(j_local * (v_pack - LANES) + 1) // LANES)) * LANES
    occ = jnp.broadcast_to(narrow(occ_labels)[:, None, None], (occ_labels.shape[0], 1, v_pack))
    sems = pltpu.SemaphoreType.DMA
    vmem = pl.BlockSpec(memory_space=pltpu.VMEM)
    return pl.pallas_call(
        functools.partial(contract_kernel, n_pair, n_fold),
        out_shape=jax.ShapeDtypeStruct((j_local, count, v_pack), jnp.float32),
        in_specs=[vmem] * 7,
        out_specs=vmem,
        scratch_shapes=[
            pltpu.VMEM((n_fold, rows, wide), moved.dtype),
            pltpu.VMEM((n_fold, n_pair, rows, wide), moved.dtype),
            pltpu.VMEM((j_local, count, v_pack), jnp.float32),
        ]
        + [pltpu.VMEM((n_outer, count, lanes), jnp.int16)] * 4
        + [
            sems, sems((n_fold,)), sems((n_fold,)), sems((n_fold, n_y)), sems((n_fold, n_y)),
            sems((n_fold, n_y)), sems((n_fold, n_y)),
            sems((n_outer,)), sems((n_outer,)), sems((n_outer,)), sems((n_outer,)),
        ],
        compiler_params=pltpu.CompilerParams(
            collective_id=0, has_side_effects=True, vmem_limit_bytes=56 << 20
        ),
    )(occ, own_labels[:, None], vir_labels.reshape(FOLDS, 1, v_pack), narrow(row_labels), narrow(col_labels), moved, packed_w)


def body(n_pair, n_fold, amplitudes, cycle_block, occ_sizes, vir_sizes, window_i, window_occ):
    c_local, occ_total, j_local, vir_total = cycle_block.shape
    n_i, k_local, a_rows, _ = amplitudes.shape
    v_pack = vir_total // FOLDS
    k_pack = occ_total // FOLDS
    rows = n_i * a_rows // n_pair
    fold = lax.axis_index("fold")
    pair = lax.axis_index("pair")
    occ_labels = irrep_labels(occ_sizes, occ_total)
    vir_labels = irrep_labels(vir_sizes, vir_total)
    c_labels = lax.dynamic_slice_in_dim(vir_labels, fold * c_local, c_local)
    a_labels = lax.dynamic_slice_in_dim(vir_labels, fold * a_rows, a_rows)
    k_labels = lax.dynamic_slice_in_dim(occ_labels, pair * k_local, k_local)
    i_labels = label_lookup(window_i, occ_labels, occ_total)
    j_orbitals = lax.dynamic_slice_in_dim(window_occ, pair * j_local, j_local)
    j_labels = label_lookup(j_orbitals, occ_labels, occ_total)

    parts = pack_t(amplitudes, i_labels[:, None] ^ k_labels[None, :], a_labels, vir_labels, n_pair)
    moved = lax.all_to_all(parts, "pair", split_axis=0, concat_axis=0, tiled=True)
    packed_w = pack_w(cycle_block, occ_labels, c_labels[:, None] ^ j_labels[None, :], vir_labels)

    ia_labels = (i_labels[:, None] ^ a_labels[None, :]).reshape(n_pair, rows)
    own_labels = lax.dynamic_slice_in_dim(ia_labels, pair, 1)[0]
    row_labels = (vir_labels.reshape(n_fold, 1, a_rows) ^ i_labels[None, :, None]).reshape(n_fold, -1, 1)
    col_labels = (occ_labels[:, None] ^ c_labels[None, :]).reshape(FOLDS, 1, k_pack * c_local)
    summed = contract_all(
        n_pair, n_fold, moved, packed_w, occ_labels, own_labels, vir_labels, row_labels, col_labels
    )
    own = summed.astype(jnp.bfloat16).reshape(j_local, n_i, a_rows, v_pack).transpose(1, 2, 0, 3)
    iaj = i_labels[:, None, None] ^ a_labels[None, :, None] ^ j_labels[None, None, :]
    keep = iaj[..., None] == vir_labels
    return jnp.where(keep, jnp.concatenate([own] * FOLDS, axis=-1), 0)


def solution(mesh):
    sizes = mesh.shape["pair"], mesh.shape["fold"]
    placed = (P(None, "pair", "fold", None), P("fold", None, "pair", None), P(), P(), P(), P())

    def run(*args):
        return body(*sizes, *args)

    return jax.shard_map(
        run, mesh=mesh, in_specs=placed, out_specs=P(None, "fold", "pair", None), check_vma=False
    )
```

time: 309 us -> 149 us (0.48)
  waiting for transfers between devices: 91.3 us -> 0.01 us
  Pallas kernels: 30.7 us -> 114 us
  other arithmetic: 77.9 us -> 10.5 us
  blocking collectives: 53.2 us -> 0 us
  local copies, waits for them, and re-layouts: 33.1 us -> 17.1 us
  between operations: 13.6 us -> 0.11 us
    pallas_call x2 -> x3, Pallas kernels: 30.7 us -> 114 us  [the longest x1 89.6 us: contract_all(): pl.pallas_call(functools.partial(contract_kernel, n_pair, n_fold), out_sh...]
    unnamed x3 -> x0, waiting for transfers between devices: 74.5 us -> none
    add x3 -> x0, other arithmetic: 65.7 us -> none  [the longest x2 56.1 us: pack_slices(): folded = folded + jnp.where(keep, block[..., cut], 0)]
    all_to_all x1 -> x0, blocking collectives: 53.2 us -> none  [body(): lax.all_to_all(packed_k, 'fold', split_axis=0, concat_axis=0, tiled=True)]
    transpose x4 -> x0, local copies, waits for them, and re-layouts: 17.6 us -> none  [the longest x2 14.3 us: pack_slices(): block = source[:, s * k_pack:(s + 1) * k_pack].transpose(2, 1, 0, 3)]
    all_gather x1 -> x0, waiting for transfers between devices: 16.8 us -> none  [body(): gathered = lax.all_gather(relaid, 'pair', axis=0, tiled=False)]
    unnamed x11 -> x12, local copies, waits for them, and re-layouts: 3.57 us -> 12.1 us
    add x5 -> x0, local copies, waits for them, and re-layouts: 6.23 us -> none  [the longest x4 3.7 us: pack_slices(): folded = folded + jnp.where(keep, block[..., cut], 0)]
  transfers between devices with their start and end apart: 3 -> 1, of which waited for: 2 -> 0; matrix products, arithmetic and copies ran while one was open for 27% -> 4% of each run, Pallas kernels for 0% -> 11%
where the time goes in v1:
time: 149 us; the launch traced here: 146 us
  Pallas kernels  114 us (77%)
  local copies, waits for them, and re-layouts  17.1 us (11%)
  other arithmetic  10.5 us (7%)
  starting transfers between devices  4.38 us (3%)
    pallas_call x1, Pallas kernels, contract_all(): pl.pallas_call(functools.partial(contract_kernel, n_pair, n_fold), out_sh...  89.6 us
    pallas_call x1, Pallas kernels, pack_w(): pl.pallas_call(pack_w_kernel, grid=(occ_total // ks,), out_shape=jax.Shap...  16.3 us
    unnamed x12, local copies, waits for them, and re-layouts  12.1 us
    pallas_call x1, Pallas kernels, pack_t(): pl.pallas_call(pack_t_kernel, grid=(n_pair,), out_shape=jax.ShapeDtypeStr...  8.47 us
    select_n x1, other arithmetic, body(): return jnp.where(keep, jnp.concatenate([own] * FOLDS, axis=-1), 0)  4.46 us
    all_to_all x1, starting transfers between devices, body(): lax.all_to_all(parts, 'pair', split_axis=0, concat_axis=0, tiled=True)  4.38 us
  transfers between devices with their start and end apart: 1, of which 0 were waited for; matrix products, arithmetic and copies ran while one was open for 4% of the time, Pallas kernels for 11%

profile of v1, /device:TPU:17, one launch (start us, length us, event | category | flops | bytes accessed | tf_op | source)
XLA Modules:
  0.0 146.4 jit_solution(9849865398368701261)
XLA Ops:
  0.0 0.8 reduce-window.16
  0.8 0.1 convert_reduce_fusion.1.occ_ref
  0.9 0.8 reduce-window.17
  1.7 0.1 convert_reduce_fusion
  1.9 0.1 convert_bitcast_fusion
  1.9 0.8 select_reduce_fusion
  2.8 0.1 dynamic_slice.16
  2.8 0.1 broadcast_xor_fusion.1
  2.9 0.1 xor.158.label_ref
  3.0 0.1 copy.26.row_ref
  3.1 0.0 copy-start.2
  3.1 3.3 %copy-done.2 = bf16[4,20,80,640]{3,2,1,0:T(8,128)(2,1)S(1)} copy-done((bf16[4,20,80,640]{3,2,1,0:T(8,128)(2,1)S(1)}, bf16[4,20,80,640]{3,2,1,0:T(8,128)(2,1)}, u32[]{:S(2)}) %copy-start.2) | copy-done | bytes 8192024
  6.5 8.5 %shard_map.64 = bf16[4,25,80,128]{3,2,1,0:T(8,128)(2,1)} custom-call(s32[80]{0:T(128)S(1)} %xor.158.label_ref, bf16[1,80,1]{2,1,0:T(8,128)(2,1)S(1)} %copy.26.row_ref, s32[1,640]{1,0:T(1,128)S(1)} %broadcast_in_dim.36.vir_ref, bf16[4,20,1,80,640]{4,3,2,1,0:T(8,128)(2,1)S(1)} %bitcast.13), custom_call_target="tpu_custom_call" | custom-call | tf_op jit(solution)/shard_map/pallas_call | solution.py:66
  14.9 0.0 copy-start.5
  14.9 4.4 %all-to-all-start = ((bf16[4,25,80,128]{3,2,1,0:T(8,128)(2,1)}), bf16[4,25,80,128]{3,2,1,0:T(8,128)(2,1)S(1)}, u32[]{:S(2)}, u32[]{:S(2)}) async-start(bf16[4,25,80,128]{3,2,1,0:T(8,128)(2,1)} %shard_map.64), calls=%async_computation | async-start | bytes 4096000 | tf_op jit(solution)/shard_map/all_to_all | solution.py:448
  19.3 0.1 broadcast_xor_fusion.2
  19.4 0.7 reshape.253.vir_ref
  20.1 0.1 xor.142
  20.1 0.1 xor.148
  20.2 0.7 copy.29.own_ref
  20.9 0.6 xor.162
  21.5 0.1 xor.136
  21.6 0.1 xor.145
  21.7 0.1 xor.149
  21.8 0.7 xor.163
  22.5 0.1 xor.152
  22.6 0.0 copy-done.5
  22.6 0.1 dynamic_slice.14
  22.7 0.2 fusion
  22.8 0.1 convert_convert_fusion.2
  22.9 0.1 copy.27
  23.0 0.1 convert_element_type.97.row_ref
  23.1 0.0 copy-start.1
  23.1 5.6 %copy-done.1 = bf16[80,80,2,640]{3,2,1,0:T(2,128)(2,1)S(1)} copy-done((bf16[80,80,2,640]{3,2,1,0:T(2,128)(2,1)S(1)}, bf16[80,80,2,640]{3,2,1,0:T(2,128)(2,1)}, u32[]{:S(2)}) %copy-start.1) | copy-done | bytes 16384024
  28.8 16.3 %shard_map.65.w_ref = bf16[2,6400,160]{2,1,0:T(8,128)(2,1)S(1)} custom-call(s32[80]{0:T(128)S(1)} %convert_reduce_fusion.1.occ_ref, bf16[160,1]{1,0:T(8,128)(2,1)S(1)} %convert_element_type.97.row_ref, s32[1,640]{1,0:T(1,128)S(1)} %broadcast_in_dim.36.vir_ref, bf16[80,80,2,640]{3,2,1,0:T(2,128)(2,1)S(1)} %copy-done.1), custom_call_target="tpu_custom_call" | custom-call | bytes 32768000 | tf_op jit(solution)/shard_map/pallas_call | solution.py:101
  45.1 0.0 copy-start
  45.1 2.7 %copy-done = bf16[2,6400,160]{2,1,0:T(8,128)(2,1)} copy-done((bf16[2,6400,160]{2,1,0:T(8,128)(2,1)}, bf16[2,6400,160]{2,1,0:T(8,128)(2,1)S(1)}, u32[]{:S(2)}) %copy-start) | copy-done | bytes 4096024
  47.8 0.1 broadcast_xor_fusion
  47.9 1.0 convert_convert_fusion.row_ref
  48.9 0.0 copy-done.4
  48.9 0.6 convert_convert_fusion.1.col_ref
  49.6 0.0 all-to-all-done.moved_ref
  49.6 1.0 broadcast_in_dim.35.occ_ref
  50.5 0.4 copy-done.3
  50.9 89.6 %shard_map.66 = f32[2,320,160]{2,1,0:T(8,128)} custom-call(bf16[80,1,160]{2,1,0:T(2,128)(2,1)} %broadcast_in_dim.35.occ_ref, s32[80,1]{1,0:T(8,128)} %copy.29.own_ref, s32[4,1,160]{2,1,0:T(1,128)} %reshape.253.vir_ref, bf16[8,320,1]{2,1,0:T(8,128)(2,1)} %convert_convert_fusion.row_ref, bf16[4,1,1600]{2,1,0:T(2,128)(2,1)} %convert_convert_fusion.1.col_ref, ...), custom_call_target="tpu_custom_call" | custom-call | tf_op jit(solution)/shard_map/pallas_call | solution.py:408
  140.5 1.1 convert_element_type.96
  141.6 0.3 copy.32
  142.0 4.5 %compare_select_fusion = bf16[4,80,2,640]{3,2,1,0:T(2,128)(2,1)} fusion(bf16[4,80,2,160]{3,2,1,0:T(2,128)(2,1)S(1)} %bitcast.14, s32[640]{0:T(1024)S(1)} %convert_reduce_fusion, s32[4,80,2]{2,1,0:T(8,128)S(1)} %broadcast_xor_fusion), kind=kLoop, calls=%fused_computation | loop fusion | flops 4096000 | bytes 1029120 | tf_op jit(solution)/shard_map/jit(_where)/select_n | solution.py:461
  (7 shorter events, 0.0 us)
Async XLA Ops:
  3.1 3.3 %copy-start.2 = (bf16[4,20,80,640]{3,2,1,0:T(8,128)(2,1)S(1)}, bf16[4,20,80,640]{3,2,1,0:T(8,128)(2,1)}, u32[]{:S(2)}) copy-start(bf16[4,20,80,640]{3,2,1,0:T(8,128)(2,1)} %param.6) | copy-start | bytes 24576004
  14.9 7.7 %copy-start.5 = (s32[8]{0:T(128)S(1)}, s32[8]{0:T(128)}, u32[]{:S(2)}) copy-start(s32[8]{0:T(128)} %param.11) | copy-start | bytes 100
  14.9 34.6 %all-to-all-start = ((bf16[4,25,80,128]{3,2,1,0:T(8,128)(2,1)}), bf16[4,25,80,128]{3,2,1,0:T(8,128)(2,1)S(1)}, u32[]{:S(2)}, u32[]{:S(2)}) async-start(bf16[4,25,80,128]{3,2,1,0:T(8,128)(2,1)} %shard_map.64), calls=%async_computation | async-start | bytes 4096000 | tf_op jit(solution)/shard_map/all_to_all | solution.py:448
  23.1 5.7 %copy-start.1 = (bf16[80,80,2,640]{3,2,1,0:T(2,128)(2,1)S(1)}, bf16[80,80,2,640]{3,2,1,0:T(2,128)(2,1)}, u32[]{:S(2)}) copy-start(bf16[80,80,2,640]{3,2,1,0:T(2,128)(2,1)} %w_ref.1) | copy-start | bytes 49152004
  45.1 2.7 %copy-start = (bf16[2,6400,160]{2,1,0:T(8,128)(2,1)}, bf16[2,6400,160]{2,1,0:T(8,128)(2,1)S(1)}, u32[]{:S(2)}) copy-start(bf16[2,6400,160]{2,1,0:T(8,128)(2,1)S(1)} %shard_map.65.w_ref) | copy-start | bytes 12288004
  47.8 1.2 copy-start.4
  49.6 1.3 copy-start.3

commit v2 on v1

v2 whole, which is shorter than its diff:
```python
import functools
import math

import jax
import jax.numpy as jnp
from jax import lax
from jax.experimental import pallas as pl
from jax.experimental.pallas import tpu as pltpu
from jax.sharding import PartitionSpec as P

LANES = 128
FOLDS = 4
AHEAD = 3
STEPS = 32000.0
FINE = 8.0


def irrep_labels(sizes, count):
    boundaries = jnp.cumsum(sizes)
    positions = jnp.arange(count, dtype=jnp.int32)
    return jnp.sum((positions[:, None] >= boundaries[None, :]).astype(jnp.int32), axis=1)


def label_lookup(orbitals, labels, count):
    matches = orbitals[:, None] == jnp.arange(count, dtype=jnp.int32)[None, :]
    return jnp.sum(jnp.where(matches, labels[None, :], 0), axis=1)


def narrow(labels):
    return labels.astype(jnp.float32).astype(jnp.bfloat16)


def fold_columns(values, rows, lanes):
    v_pack = values.shape[1] // FOLDS
    total = jnp.zeros((values.shape[0], v_pack), values.dtype)
    for q in range(FOLDS):
        cut = slice(q * v_pack, (q + 1) * v_pack)
        total = jnp.where(rows == lanes[:, cut], values[:, cut], total)
    return total


def pack_t_kernel(label_ref, row_ref, vir_ref, t_ref, out_ref):
    piece = pl.program_id(0)
    k_local = t_ref.shape[1]
    rest = t_ref.shape[-1] // FOLDS - LANES
    group = LANES // rest
    tails = []
    for k in range(k_local):
        lanes = narrow(vir_ref[...] ^ label_ref[piece * k_local + k])
        total = fold_columns(t_ref[0, k, 0], row_ref[0], lanes)
        base = k // group * (group + 1)
        out_ref[0, base + k % group] = total[:, :LANES]
        tails.append(total[:, LANES:])
        if k == k_local - 1:
            tails += [jnp.zeros_like(tails[0])] * (group - len(tails))
        if len(tails) == group:
            out_ref[0, base + group] = jnp.concatenate(tails, axis=1)
            tails = []


def pack_t(amplitudes, ik_labels, a_labels, vir_labels, n_pair):
    n_i, k_local, a_rows, vir_total = amplitudes.shape
    split = n_pair // n_i
    rows = a_rows // split
    group = LANES // (vir_total // FOLDS - LANES)
    slabs = -(-k_local // group) * (group + 1)
    source = amplitudes.reshape(n_i, k_local, split, rows, vir_total)
    labels = jnp.broadcast_to(ik_labels[:, None, :], (n_i, split, k_local)).reshape(-1)
    return pl.pallas_call(
        pack_t_kernel,
        grid=(n_pair,),
        out_shape=jax.ShapeDtypeStruct((n_pair, slabs, rows, LANES), amplitudes.dtype),
        in_specs=[
            pl.BlockSpec(memory_space=pltpu.SMEM),
            pl.BlockSpec((1, rows, 1), lambda p: (p % split, 0, 0)),
            pl.BlockSpec((1, vir_total), lambda p: (0, 0)),
            pl.BlockSpec((1, k_local, 1, rows, vir_total), lambda p: (p // split, 0, p % split, 0, 0)),
        ],
        out_specs=pl.BlockSpec((1, slabs, rows, LANES), lambda p: (p, 0, 0, 0)),
        compiler_params=pltpu.CompilerParams(vmem_limit_bytes=32 << 20),
    )(labels, narrow(a_labels).reshape(split, rows, 1), vir_labels[None, :], source)


def flip(index, bits, count):
    total, bit = 0, 1
    while bit < count:
        total = total + (index // bit + bits // bit) % 2 * bit
        bit *= 2
    return total


def encode(parts, out_ref):
    top = functools.reduce(jnp.maximum, [jnp.max(jnp.abs(part), axis=1, keepdims=True) for part in parts])
    code = jnp.ceil(jnp.log2(jnp.maximum(top, 1e-30)) * FINE)
    factor = STEPS * jnp.exp2(code * (-1.0 / FINE))
    scaled = [jnp.round(part * factor).astype(jnp.int32) for part in parts]
    rest = [part[:, LANES:] for part in scaled]
    spare = LANES - sum(part.shape[1] for part in rest)
    rest.append(jnp.broadcast_to(code.astype(jnp.int32), (code.shape[0], spare)))
    for j, part in enumerate(scaled):
        out_ref[:, j * LANES:(j + 1) * LANES] = part[:, :LANES].astype(jnp.int16)
    out_ref[:, len(parts) * LANES:] = jnp.concatenate(rest, axis=1).astype(jnp.int16)


def decode(packed, count, width):
    values = packed.astype(jnp.int32).astype(jnp.float32)
    code = values[:, -1:]
    values = values * (jnp.exp2(code * (1.0 / FINE)) / STEPS)
    rest = width - LANES
    return [
        jnp.concatenate(
            [
                values[:, j * LANES:(j + 1) * LANES],
                values[:, count * LANES + j * rest:count * LANES + (j + 1) * rest],
            ],
            axis=1,
        )
        for j in range(count)
    ]


def spans_of(k_pack, c_local):
    step = LANES // math.gcd(LANES, c_local)
    return [(0, step), (step, k_pack - step)]


def cycle_kernel(
    n_pair, n_fold, label_ref, occ_ref, own_ref, vir_ref, line_ref, cj_ref, row_ref, col_ref, parts_ref, w_hbm,
    out_ref, moved, wide, held, packed_w, raw_w, main_w, rest_w, total, x_out, x_in, z_out, z_in,
    copy_sem, w_sem, a_send, a_recv, f_send, f_recv, y_send, y_recv, c_send, c_recv,
    x_send, x_recv, z_send, z_recv,
):
    pair, fold = lax.axis_index("pair"), lax.axis_index("fold")
    n_y, n_outer, here = n_pair // 2, n_fold // 2, n_fold // FOLDS
    y, core = pair // 2, pair % 2
    outer, half = fold // 2, fold % 2
    mate = y * 2 + 1 - core
    rows, v_pack = own_ref.shape[0], vir_ref.shape[2]
    c_local, occ_total, j_local, vir_total = w_hbm.shape
    k_pack, k_local = occ_total // FOLDS, occ_total // n_pair
    rest = v_pack - LANES
    group = LANES // rest
    spans = spans_of(k_pack, c_local)
    chunks = len(spans)
    lanes_of = [
        (first * c_local, -(-count * c_local // LANES) * LANES) for first, count in spans
    ]
    slabs = moved.shape[1]
    if k_local == k_pack:
        slabs_of = [
            (first // group * (group + 1), -(-count // group) * (group + 1)) for first, count in spans
        ]
    else:
        slabs_of = [(0, slabs)] + [None] * (chunks - 1)

    barrier = pltpu.get_barrier_semaphore()
    for step in range(1, n_fold):
        pl.semaphore_signal(barrier, device_id={"fold": (fold + step) % n_fold})
    for step in range(1, n_pair):
        pl.semaphore_signal(barrier, device_id={"pair": (pair + step) % n_pair})
    pl.semaphore_wait(barrier, n_fold + n_pair - 2)

    def to_pair(step, chunk):
        other = (pair + step) % n_pair
        first, count = slabs_of[chunk]
        return pltpu.make_async_remote_copy(
            src_ref=parts_ref.at[other, pl.ds(first, count)],
            dst_ref=moved.at[pair, pl.ds(first, count)],
            send_sem=a_send.at[other, chunk], recv_sem=a_recv.at[pair, chunk],
            device_id={"pair": other},
        )

    def from_pair(step, chunk):
        other = (pair + step) % n_pair
        first, count = slabs_of[chunk]
        return pltpu.make_async_remote_copy(
            src_ref=parts_ref.at[other, pl.ds(first, count)],
            dst_ref=moved.at[other, pl.ds(first, count)],
            send_sem=a_send.at[other, chunk], recv_sem=a_recv.at[other, chunk],
            device_id={"pair": other},
        )

    def piece_of(ref, index, chunk):
        return ref.at[(*index, slice(None), pl.ds(*lanes_of[chunk]))]

    def to_fold(target, chunk):
        return pltpu.make_async_remote_copy(
            src_ref=piece_of(wide, (target,), chunk), dst_ref=piece_of(held, (fold, pair), chunk),
            send_sem=f_send.at[target, chunk], recv_sem=f_recv.at[fold, chunk],
            device_id={"fold": target},
        )

    def from_fold(source, chunk):
        return pltpu.make_async_remote_copy(
            src_ref=piece_of(wide, (source,), chunk), dst_ref=piece_of(held, (source, pair), chunk),
            send_sem=f_send.at[source, chunk], recv_sem=f_recv.at[source, chunk],
            device_id={"fold": source},
        )

    def shared(source, other, whose, sends, recvs, mark, chunk, target):
        slot = piece_of(held, (source, whose), chunk)
        return pltpu.make_async_remote_copy(
            src_ref=slot, dst_ref=slot,
            send_sem=sends.at[source, other, chunk], recv_sem=recvs.at[source, mark, chunk],
            device_id={"pair": target},
        )

    def over_y(source, step, chunk):
        other = (y + step) % n_y
        return shared(source, other, pair, y_send, y_recv, y, chunk, other * 2 + core)

    def from_y(source, step, chunk):
        other = (y + step) % n_y
        target = other * 2 + core
        return shared(source, other, target, y_send, y_recv, other, chunk, target)

    def over_core(source, step, chunk):
        other = (y + step) % n_y
        return shared(source, other, other * 2 + core, c_send, c_recv, other, chunk, mate)

    def from_core(source, step, chunk):
        other = (y + step) % n_y
        return shared(source, other, other * 2 + 1 - core, c_send, c_recv, other, chunk, mate)

    def over_x(block):
        return pltpu.make_async_remote_copy(
            src_ref=x_out.at[block], dst_ref=x_in.at[block],
            send_sem=x_send.at[block], recv_sem=x_recv.at[block],
            device_id={"fold": outer * 2 + 1 - half},
        )

    def over_z(block, slot):
        return pltpu.make_async_remote_copy(
            src_ref=z_out.at[block], dst_ref=z_in.at[slot],
            send_sem=z_send.at[block], recv_sem=z_recv.at[slot],
            device_id={"fold": block * 2 + half},
        )

    def own_parts():
        return pltpu.make_async_copy(parts_ref.at[pair], moved.at[pair], copy_sem)

    loads = raw_w.shape[2]
    n_loads = occ_total // loads

    def load_w(step):
        slot = step % 2
        return pltpu.make_async_copy(
            w_hbm.at[:, pl.ds(step * loads, loads)], raw_w.at[slot], w_sem.at[slot]
        )

    def pack_w(step, carry):
        load_w(step).wait()
        slot = step % 2
        for k in range(loads):
            lanes = narrow(line_ref[...] ^ label_ref[step * loads + k])
            values = raw_w[slot, :, k].reshape(c_local * j_local, vir_total)
            chosen = fold_columns(values, cj_ref[...], lanes).astype(jnp.float32)
            main_w[...] = chosen[:, :LANES]
            rest_w[:, :rest] = chosen[:, LANES:]
            block = step * (loads // 4) + k // 4
            place = slice(k % 4 * c_local, (k % 4 + 1) * c_local)
            for j in range(j_local):
                own = pl.ds(j, c_local, stride=j_local)
                packed_w[j, block, place, :LANES] = main_w[own, :].astype(packed_w.dtype)
                packed_w[j, block, place, LANES:] = rest_w[own, :][:, :rest].astype(packed_w.dtype)

        @pl.when(step + 2 < n_loads)
        def _():
            load_w(step + 2).start()

        return carry

    def source_of(step):
        return flip(outer, step // 2, n_outer) * 2 + (half + 1 + step) % 2

    def relay(source, chunk):
        for step in range(1, n_y):
            over_y(source, step, chunk).start()
        over_core(source, 0, chunk).start()

    def fetch(step, chunk):
        source = source_of(step)

        @pl.when(step != 1)
        def _():
            from_fold(source, chunk).wait_recv()
            relay(source, chunk)

    def pass_on(step, chunk):
        source = source_of(step)
        for other in range(1, n_y):
            from_y(source, other, chunk).wait_recv()
            over_core(source, other, chunk).start()

    def pack_k(chunk):
        first, count = spans[chunk]
        start, width = lanes_of[chunk]
        if slabs_of[chunk] is not None:
            for step in range(1, n_pair):
                from_pair(step, chunk).wait_recv()

        def quarter(step, carry):
            q = flip(fold // here, step, FOLDS)
            labels = narrow(own_ref[...] ^ vir_ref[q])
            pieces = [[] for _ in range(here)]
            for kappa in range(first, first + count):
                chosen = jnp.zeros((rows, v_pack), moved.dtype)
                for s in range(FOLDS):
                    k = s * k_pack + kappa
                    side, inner = k // k_local, k % k_local
                    base, tail = inner // group * (group + 1), inner % group * rest
                    piece = jnp.concatenate(
                        [moved[side, base + inner % group], moved[side, base + group][:, tail:tail + rest]],
                        axis=1,
                    )
                    chosen = jnp.where(labels == occ_ref[k], piece, chosen)
                for f in range(here):
                    pieces[f].append(chosen[:, f * c_local:(f + 1) * c_local])
            spare = width - count * c_local
            for f in range(here):
                if spare:
                    pieces[f].append(jnp.zeros((rows, spare), moved.dtype))
                wide[q * here + f, :, start:start + width] = jnp.concatenate(pieces[f], axis=1)
            for f in range(here):

                @pl.when(step * here + f > 0)
                def _():
                    to_fold(q * here + (fold + f) % here, chunk).start()

            return carry

        lax.fori_loop(0, FOLDS, quarter, 0)
        own = pltpu.make_async_copy(
            piece_of(wide, (fold,), chunk), piece_of(held, (fold, pair), chunk), copy_sem
        )
        own.start()
        own.wait()
        relay(fold, chunk)

    def multiply(step, chunk):
        source = source_of(step)
        block = flip(outer, step // 2, n_outer)
        first, count = spans[chunk]
        start, depth = first * c_local, count * c_local
        for other in range(n_y):
            from_core(source, other, chunk).wait_recv()
        left = jnp.concatenate([held[source, p, :, start:start + depth] for p in range(n_pair)], axis=0)
        labels = row_ref[source]
        sums = [None] * j_local
        if chunk:
            sums = [total[source, j] for j in range(j_local)]
        for s in range(FOLDS):
            part = jnp.where(labels == col_ref[s, :, start:start + depth], left, jnp.zeros_like(left))
            place = (s * k_pack + first) // 4
            for j in range(j_local):
                right = packed_w[j, place:place + count // 4].reshape(depth, v_pack)
                term = jnp.dot(part, right, preferred_element_type=jnp.float32)
                sums[j] = term if sums[j] is None else sums[j] + term
        for j in range(j_local):
            total[source, j] = sums[j]
        if chunk < chunks - 1:
            return

        @pl.when(step % 2 == 0)
        def _():
            encode([total[source, j] for j in range(j_local)], x_out.at[block])
            over_x(block).start()

        @pl.when(step % 2 == 1)
        def _():
            over_x(block).wait_recv()
            near = decode(x_in[block], j_local, v_pack)
            near = [total[source, j] + near[j] for j in range(j_local)]

            @pl.when(step == 1)
            def _():
                for j in range(j_local):
                    out_ref[j] = near[j]

            @pl.when(step > 1)
            def _():
                encode(near, z_out.at[block])
                over_z(block, outer).start()

    for chunk in range(chunks):
        if slabs_of[chunk] is not None:
            for step in range(1, n_pair):
                to_pair(step, chunk).start()
    own_parts().start()
    load_w(0).start()
    load_w(1).start()
    own_parts().wait()
    lax.fori_loop(0, n_loads // 2, pack_w, 0)
    pack_k(0)
    lax.fori_loop(n_loads // 2, n_loads, pack_w, 0)
    for chunk in range(1, chunks):
        pack_k(chunk)

    for step in range(AHEAD):
        fetch(step, 0)
    pass_on(0, 0)
    for chunk in range(chunks):

        def source_step(step, carry):
            @pl.when(step + AHEAD < n_fold)
            def _():
                fetch(step + AHEAD, chunk)

            @pl.when(step + 1 < n_fold)
            def _():
                pass_on(step + 1, chunk)

            if chunk < chunks - 1:

                @pl.when(step + AHEAD >= n_fold)
                def _():
                    fetch(step + AHEAD - n_fold, chunk + 1)

                @pl.when(step + 1 >= n_fold)
                def _():
                    pass_on(step + 1 - n_fold, chunk + 1)

            multiply(step, chunk)
            return carry

        lax.fori_loop(0, n_fold, source_step, 0)

    def finish(step, carry):
        block = flip(outer, step, n_outer)
        over_z(block, block).wait_recv()
        far = decode(z_in[block], j_local, v_pack)
        for j in range(j_local):
            out_ref[j] += far[j]
        return carry

    lax.fori_loop(1, n_outer, finish, 0)

    for chunk in range(chunks):
        if slabs_of[chunk] is not None:
            for step in range(1, n_pair):
                to_pair(step, chunk).wait_send()

        def drain(source, carry):
            @pl.when(source != fold)
            def _():
                to_fold(source, chunk).wait_send()

            for step in range(1, n_y):
                over_y(source, step, chunk).wait_send()
            for step in range(n_y):
                over_core(source, step, chunk).wait_send()
            return carry

        lax.fori_loop(0, n_fold, drain, 0)

    def drain_sums(block, carry):
        over_x(block).wait_send()

        @pl.when(block != outer)
        def _():
            over_z(block, outer).wait_send()

        return carry

    lax.fori_loop(0, n_outer, drain_sums, 0)


def contract_all(
    n_pair, n_fold, parts, cycle_block, occ_labels, own_labels, vir_labels, cj_labels, row_labels, col_labels
):
    _, slabs, rows, _ = parts.shape
    c_local, occ_total, j_local, vir_total = cycle_block.shape
    v_pack = vir_total // FOLDS
    depth = col_labels.shape[-1]
    wide = -(-depth // LANES) * LANES
    n_y, n_outer = n_pair // 2, n_fold // 2
    count = n_pair * rows
    lanes = (j_local + -(-(j_local * (v_pack - LANES) + 1) // LANES)) * LANES
    chunks = len(spans_of(occ_total // FOLDS, c_local))
    loads = 8
    occ = jnp.broadcast_to(narrow(occ_labels)[:, None, None], (occ_total, 1, v_pack))
    sems = pltpu.SemaphoreType.DMA
    vmem = pl.BlockSpec(memory_space=pltpu.VMEM)
    kind = parts.dtype
    return pl.pallas_call(
        functools.partial(cycle_kernel, n_pair, n_fold),
        out_shape=jax.ShapeDtypeStruct((j_local, count, v_pack), jnp.float32),
        in_specs=[pl.BlockSpec(memory_space=pltpu.SMEM)] + [vmem] * 8 + [pl.BlockSpec(memory_space=pl.ANY)],
        out_specs=vmem,
        scratch_shapes=[
            pltpu.VMEM(parts.shape, kind),
            pltpu.VMEM((n_fold, rows, wide), kind),
            pltpu.VMEM((n_fold, n_pair, rows, wide), kind),
            pltpu.VMEM((j_local, occ_total // 4, 4 * c_local, v_pack), kind),
            pltpu.VMEM((2, c_local, loads, j_local, vir_total), kind),
            pltpu.VMEM((c_local * j_local, LANES), jnp.float32),
            pltpu.VMEM((c_local * j_local, LANES), jnp.float32),
            pltpu.VMEM((n_fold, j_local, count, v_pack), jnp.float32),
        ]
        + [pltpu.VMEM((n_outer, count, lanes), jnp.int16)] * 4
        + [
            sems, sems((2,)), sems((n_pair, chunks)), sems((n_pair, chunks)),
            sems((n_fold, chunks)), sems((n_fold, chunks)),
            sems((n_fold, n_y, chunks)), sems((n_fold, n_y, chunks)),
            sems((n_fold, n_y, chunks)), sems((n_fold, n_y, chunks)),
            sems((n_outer,)), sems((n_outer,)), sems((n_outer,)), sems((n_outer,)),
        ],
        compiler_params=pltpu.CompilerParams(
            collective_id=0, has_side_effects=True, vmem_limit_bytes=56 << 20
        ),
    )(
        occ_labels, occ, own_labels[:, None], vir_labels.reshape(FOLDS, 1, v_pack), vir_labels[None, :],
        narrow(cj_labels).reshape(-1, 1), narrow(row_labels), narrow(col_labels), parts, cycle_block,
    )


def body(n_pair, n_fold, amplitudes, cycle_block, occ_sizes, vir_sizes, window_i, window_occ):
    c_local, occ_total, j_local, vir_total = cycle_block.shape
    n_i, k_local, a_rows, _ = amplitudes.shape
    v_pack = vir_total // FOLDS
    k_pack = occ_total // FOLDS
    rows = n_i * a_rows // n_pair
    fold = lax.axis_index("fold")
    pair = lax.axis_index("pair")
    occ_labels = irrep_labels(occ_sizes, occ_total)
    vir_labels = irrep_labels(vir_sizes, vir_total)
    c_labels = lax.dynamic_slice_in_dim(vir_labels, fold * c_local, c_local)
    a_labels = lax.dynamic_slice_in_dim(vir_labels, fold * a_rows, a_rows)
    k_labels = lax.dynamic_slice_in_dim(occ_labels, pair * k_local, k_local)
    i_labels = label_lookup(window_i, occ_labels, occ_total)
    j_orbitals = lax.dynamic_slice_in_dim(window_occ, pair * j_local, j_local)
    j_labels = label_lookup(j_orbitals, occ_labels, occ_total)

    parts = pack_t(amplitudes, i_labels[:, None] ^ k_labels[None, :], a_labels, vir_labels, n_pair)
    ia_labels = (i_labels[:, None] ^ a_labels[None, :]).reshape(n_pair, rows)
    own_labels = lax.dynamic_slice_in_dim(ia_labels, pair, 1)[0]
    row_labels = (vir_labels.reshape(n_fold, 1, a_rows) ^ i_labels[None, :, None]).reshape(n_fold, -1, 1)
    col_labels = (occ_labels[:, None] ^ c_labels[None, :]).reshape(FOLDS, 1, k_pack * c_local)
    summed = contract_all(
        n_pair, n_fold, parts, cycle_block, occ_labels, own_labels, vir_labels,
        c_labels[:, None] ^ j_labels[None, :], row_labels, col_labels,
    )
    own = summed.astype(jnp.bfloat16).reshape(j_local, n_i, a_rows, v_pack).transpose(1, 2, 0, 3)
    iaj = i_labels[:, None, None] ^ a_labels[None, :, None] ^ j_labels[None, None, :]
    keep = iaj[..., None] == vir_labels
    return jnp.where(keep, jnp.concatenate([own] * FOLDS, axis=-1), 0)


def solution(mesh):
    sizes = mesh.shape["pair"], mesh.shape["fold"]
    placed = (P(None, "pair", "fold", None), P("fold", None, "pair", None), P(), P(), P(), P())

    def run(*args):
        return body(*sizes, *args)

    return jax.shard_map(
        run, mesh=mesh, in_specs=placed, out_specs=P(None, "fold", "pair", None), check_vma=False
    )
```

time: 149 us -> 138 us (0.926)
  local copies, waits for them, and re-layouts: 17.1 us -> 10.2 us
  starting transfers between devices: 4.38 us -> 0 us
    unnamed x12 -> x8, local copies, waits for them, and re-layouts: 12.1 us -> 4.64 us
    all_to_all x1 -> x0, starting transfers between devices: 4.38 us -> none  [body(): lax.all_to_all(parts, 'pair', split_axis=0, concat_axis=0, tiled=True)]
    pallas_call x2 -> x1, Pallas kernels: 106 us -> 108 us  [contract_all(): pl.pallas_call(functools.partial(cycle_kernel, n_pair, n_fold), out_shape...]
  transfers between devices with their start and end apart: 1 -> 0, of which waited for: 0 -> 0; matrix products, arithmetic and copies ran while one was open for 4% -> 0% of each run, Pallas kernels for 11% -> 0%
where the time goes in v2:
time: 138 us; the launch traced here: 136 us
  Pallas kernels  115 us (83%)
  other arithmetic  10.5 us (8%)
  local copies, waits for them, and re-layouts  10.2 us (7%)
    pallas_call x1, Pallas kernels, contract_all(): pl.pallas_call(functools.partial(cycle_kernel, n_pair, n_fold), out_shape...  108 us
    pallas_call x1, Pallas kernels, pack_t(): pl.pallas_call(pack_t_kernel, grid=(n_pair,), out_shape=jax.ShapeDtypeStr...  7.59 us
    unnamed x8, local copies, waits for them, and re-layouts  4.64 us
    select_n x1, other arithmetic, body(): return jnp.where(keep, jnp.concatenate([own] * FOLDS, axis=-1), 0)  4.46 us

profile of v2, /device:TPU:17, one launch (start us, length us, event | category | flops | bytes accessed | tf_op | source)
XLA Modules:
  0.0 136.1 jit_solution(9633722027530785954)
XLA Ops:
  0.0 0.8 reduce-window.16
  0.8 0.1 convert_reduce_fusion.1.label_ref
  0.9 0.0 copy-start.3
  0.9 0.8 broadcast_in_dim.35.occ_ref
  1.7 0.8 reduce-window.17
  2.5 0.1 convert_reduce_fusion
  2.6 0.1 convert_bitcast_fusion
  2.7 0.8 select_reduce_fusion
  3.5 0.1 broadcast_xor_fusion.2
  3.6 0.7 copy.28.own_ref
  4.3 0.7 reshape.253.vir_ref
  5.0 0.0 copy-start.2
  5.0 0.7 dynamic_slice.14
  5.8 0.2 fusion
  5.9 0.1 convert_convert_fusion.2
  6.0 0.1 copy.22
  6.1 0.7 convert_element_type.97.cj_ref
  6.9 0.1 xor.145
  6.9 0.6 xor.162
  7.6 0.1 xor.136
  7.6 0.1 xor.148
  7.7 1.0 convert_convert_fusion.row_ref
  8.8 0.1 xor.151
  8.8 0.1 xor.152
  8.9 0.1 xor.163
  9.0 0.1 xor.155
  9.1 0.6 convert_convert_fusion.1.col_ref
  9.7 0.0 copy-done.3
  9.7 0.1 dynamic_slice.16
  9.8 0.1 broadcast_xor_fusion.1
  9.9 0.1 xor.161.label_ref
  10.0 0.1 copy.27.row_ref
  10.1 0.0 copy-done.2
  10.1 0.0 copy-start
  10.1 3.3 %copy-done = bf16[4,20,80,640]{3,2,1,0:T(8,128)(2,1)S(1)} copy-done((bf16[4,20,80,640]{3,2,1,0:T(8,128)(2,1)S(1)}, bf16[4,20,80,640]{3,2,1,0:T(8,128)(2,1)}, u32[]{:S(2)}) %copy-start) | copy-done | bytes 8192024
  13.4 7.6 %shard_map.64.parts_ref = bf16[4,25,80,128]{3,2,1,0:T(8,128)(2,1)S(1)} custom-call(s32[80]{0:T(128)S(1)} %xor.161.label_ref, bf16[1,80,1]{2,1,0:T(8,128)(2,1)S(1)} %copy.27.row_ref, s32[1,640]{1,0:T(1,128)S(1)} %broadcast_in_dim.36.vir_ref.line_ref, bf16[4,20,1,80,640]{4,3,2,1,0:T(8,128)(2,1)S(1)} %bitcast.13), custom_call_target="tpu_custom_call" | custom-call | tf_op jit(solution)/shard_map/pallas_call | solution.py:69
  21.0 0.0 copy-start.1
  21.0 1.3 copy-done.1
  22.3 107.7 %shard_map.65 = f32[2,320,160]{2,1,0:T(8,128)} custom-call(s32[80]{0:T(128)} %copy-done.3, bf16[80,1,160]{2,1,0:T(2,128)(2,1)} %broadcast_in_dim.35.occ_ref, s32[80,1]{1,0:T(8,128)} %copy.28.own_ref, s32[4,1,160]{2,1,0:T(1,128)} %reshape.253.vir_ref, s32[1,640]{1,0:T(1,128)} %copy-done.2, bf16[160,1]{1,0:T(8,128)(2,1)} %convert_element_type.97.cj_ref, ...), custom_call_target="tpu_custom_call" | custom-call | tf_op jit(solution)/shard_map/pallas_call | solution.py:485
  130.0 1.1 convert_element_type.96
  131.2 0.3 copy.32
  131.5 0.1 broadcast_xor_fusion
  131.6 4.5 %compare_select_fusion = bf16[4,80,2,640]{3,2,1,0:T(2,128)(2,1)} fusion(bf16[4,80,2,160]{3,2,1,0:T(2,128)(2,1)S(1)} %bitcast.14, s32[640]{0:T(1024)S(1)} %convert_reduce_fusion, s32[4,80,2]{2,1,0:T(8,128)S(1)} %broadcast_xor_fusion), kind=kLoop, calls=%fused_computation | loop fusion | flops 4096000 | bytes 1029120 | tf_op jit(solution)/shard_map/jit(_where)/select_n | solution.py:546
  (5 shorter events, 0.0 us)
Async XLA Ops:
  0.9 8.8 %copy-start.3 = (s32[80]{0:T(128)}, s32[80]{0:T(128)S(1)}, u32[]{:S(2)}) copy-start(s32[80]{0:T(128)S(1)} %convert_reduce_fusion.1.label_ref) | copy-start | bytes 964
  5.0 5.1 %copy-start.2 = (s32[1,640]{1,0:T(1,128)}, s32[1,640]{1,0:T(1,128)S(1)}, u32[]{:S(2)}) copy-start(s32[1,640]{1,0:T(1,128)S(1)} %broadcast_in_dim.36.vir_ref.line_ref) | copy-start | bytes 7684
  10.1 3.3 %copy-start = (bf16[4,20,80,640]{3,2,1,0:T(8,128)(2,1)S(1)}, bf16[4,20,80,640]{3,2,1,0:T(8,128)(2,1)}, u32[]{:S(2)}) copy-start(bf16[4,20,80,640]{3,2,1,0:T(8,128)(2,1)} %param.6) | copy-start | bytes 24576004
  21.0 1.3 copy-start.1

commit v3 on v2

--- a/solution.py
+++ b/solution.py
@@ -15,15 +15,29 @@
 FINE = 8.0
 
 
-def irrep_labels(sizes, count):
-    boundaries = jnp.cumsum(sizes)
-    positions = jnp.arange(count, dtype=jnp.int32)
-    return jnp.sum((positions[:, None] >= boundaries[None, :]).astype(jnp.int32), axis=1)
-
-
-def label_lookup(orbitals, labels, count):
-    matches = orbitals[:, None] == jnp.arange(count, dtype=jnp.int32)[None, :]
-    return jnp.sum(jnp.where(matches, labels[None, :], 0), axis=1)
+def bounds_of(sizes_ref):
+    ends, total = [], 0
+    for g in range(sizes_ref.shape[0]):
+        total = total + sizes_ref[g]
+        ends.append(total)
+    return ends
+
+
+def label_of(positions, ends):
+    return functools.reduce(jnp.add, [jnp.where(positions >= end, 1, 0) for end in ends])
+
+
+def split_by(positions, count):
+    whole = jnp.floor((positions.astype(jnp.float32) + 0.5) * (1.0 / count)).astype(jnp.int32)
+    return whole, positions - whole * count
+
+
+def column(count):
+    return lax.broadcasted_iota(jnp.int32, (count, 1), 0)
+
+
+def line(count):
+    return lax.broadcasted_iota(jnp.int32, (1, count), 1)
 
 
 def narrow(labels):
@@ -37,48 +51,6 @@
         cut = slice(q * v_pack, (q + 1) * v_pack)
         total = jnp.where(rows == lanes[:, cut], values[:, cut], total)
     return total
-
-
-def pack_t_kernel(label_ref, row_ref, vir_ref, t_ref, out_ref):
-    piece = pl.program_id(0)
-    k_local = t_ref.shape[1]
-    rest = t_ref.shape[-1] // FOLDS - LANES
-    group = LANES // rest
-    tails = []
-    for k in range(k_local):
-        lanes = narrow(vir_ref[...] ^ label_ref[piece * k_local + k])
-        total = fold_columns(t_ref[0, k, 0], row_ref[0], lanes)
-        base = k // group * (group + 1)
-        out_ref[0, base + k % group] = total[:, :LANES]
-        tails.append(total[:, LANES:])
-        if k == k_local - 1:
-            tails += [jnp.zeros_like(tails[0])] * (group - len(tails))
-        if len(tails) == group:
-            out_ref[0, base + group] = jnp.concatenate(tails, axis=1)
-            tails = []
-
-
-def pack_t(amplitudes, ik_labels, a_labels, vir_labels, n_pair):
-    n_i, k_local, a_rows, vir_total = amplitudes.shape
-    split = n_pair // n_i
-    rows = a_rows // split
-    group = LANES // (vir_total // FOLDS - LANES)
-    slabs = -(-k_local // group) * (group + 1)
-    source = amplitudes.reshape(n_i, k_local, split, rows, vir_total)
-    labels = jnp.broadcast_to(ik_labels[:, None, :], (n_i, split, k_local)).reshape(-1)
-    return pl.pallas_call(
-        pack_t_kernel,
-        grid=(n_pair,),
-        out_shape=jax.ShapeDtypeStruct((n_pair, slabs, rows, LANES), amplitudes.dtype),
-        in_specs=[
-            pl.BlockSpec(memory_space=pltpu.SMEM),
-            pl.BlockSpec((1, rows, 1), lambda p: (p % split, 0, 0)),
-            pl.BlockSpec((1, vir_total), lambda p: (0, 0)),
-            pl.BlockSpec((1, k_local, 1, rows, vir_total), lambda p: (p // split, 0, p % split, 0, 0)),
-        ],
-        out_specs=pl.BlockSpec((1, slabs, rows, LANES), lambda p: (p, 0, 0, 0)),
-        compiler_params=pltpu.CompilerParams(vmem_limit_bytes=32 << 20),
-    )(labels, narrow(a_labels).reshape(split, rows, 1), vir_labels[None, :], source)
 
 
 def flip(index, bits, count):
@@ -125,9 +97,10 @@
 
 
 def cycle_kernel(
-    n_pair, n_fold, label_ref, occ_ref, own_ref, vir_ref, line_ref, cj_ref, row_ref, col_ref, parts_ref, w_hbm,
-    out_ref, moved, wide, held, packed_w, raw_w, main_w, rest_w, total, x_out, x_in, z_out, z_in,
-    copy_sem, w_sem, a_send, a_recv, f_send, f_recv, y_send, y_recv, c_send, c_recv,
+    n_pair, n_fold, occ_sizes, vir_sizes, window_i, window_occ, t_hbm, w_hbm, out_ref,
+    occ_wide, occ_short, col_ref, cj_ref, parts, raw_t, moved, wide, held, packed_w, raw_w, main_w, rest_w,
+    total, kept, x_out, x_in, z_out, z_in,
+    copy_sem, t_sem, w_sem, a_send, a_recv, f_send, f_recv, y_send, y_recv, c_send, c_recv,
     x_send, x_recv, z_send, z_recv,
 ):
     pair, fold = lax.axis_index("pair"), lax.axis_index("fold")
@@ -135,8 +108,9 @@
     y, core = pair // 2, pair % 2
     outer, half = fold // 2, fold % 2
     mate = y * 2 + 1 - core
-    rows, v_pack = own_ref.shape[0], vir_ref.shape[2]
     c_local, occ_total, j_local, vir_total = w_hbm.shape
+    n_i, _, split, rows, _ = t_hbm.shape
+    a_rows, v_pack = split * rows, vir_total // FOLDS
     k_pack, k_local = occ_total // FOLDS, occ_total // n_pair
     rest = v_pack - LANES
     group = LANES // rest
@@ -146,35 +120,43 @@
         (first * c_local, -(-count * c_local // LANES) * LANES) for first, count in spans
     ]
     slabs = moved.shape[1]
-    if k_local == k_pack:
-        slabs_of = [
-            (first // group * (group + 1), -(-count // group) * (group + 1)) for first, count in spans
-        ]
-    else:
-        slabs_of = [(0, slabs)] + [None] * (chunks - 1)
-
-    barrier = pltpu.get_barrier_semaphore()
-    for step in range(1, n_fold):
-        pl.semaphore_signal(barrier, device_id={"fold": (fold + step) % n_fold})
-    for step in range(1, n_pair):
-        pl.semaphore_signal(barrier, device_id={"pair": (pair + step) % n_pair})
-    pl.semaphore_wait(barrier, n_fold + n_pair - 2)
+    taken = spans if k_local == k_pack else [(0, k_local)] + [None] * (chunks - 1)
+    slabs_of = [
+        span and (span[0] // group * (group + 1), -(-span[1] // group) * (group + 1)) for span in taken
+    ]
+
+    occ_ends, vir_ends = bounds_of(occ_sizes), bounds_of(vir_sizes)
+    i_labels = [label_of(window_i[i], occ_ends) for i in range(n_i)]
+    j_labels = [label_of(window_occ[pair * j_local + j], occ_ends) for j in range(j_local)]
+    vir_line = label_of(line(vir_total), vir_ends)
+
+    def load_t(step, chunk):
+        target = turn(step)
+        first, count = taken[chunk]
+        slot = step % 2
+        return pltpu.make_async_copy(
+            t_hbm.at[target // split, pl.ds(first, count), target % split],
+            raw_t.at[slot, pl.ds(0, count)], t_sem.at[slot],
+        )
+
+    def turn(step):
+        return (y + 1 + step // 2) % n_y * 2 + (core + 1 + step) % 2
 
     def to_pair(step, chunk):
-        other = (pair + step) % n_pair
+        other = turn(step)
         first, count = slabs_of[chunk]
         return pltpu.make_async_remote_copy(
-            src_ref=parts_ref.at[other, pl.ds(first, count)],
+            src_ref=parts.at[other, pl.ds(first, count)],
             dst_ref=moved.at[pair, pl.ds(first, count)],
             send_sem=a_send.at[other, chunk], recv_sem=a_recv.at[pair, chunk],
             device_id={"pair": other},
         )
 
     def from_pair(step, chunk):
-        other = (pair + step) % n_pair
+        other = turn(step)
         first, count = slabs_of[chunk]
         return pltpu.make_async_remote_copy(
-            src_ref=parts_ref.at[other, pl.ds(first, count)],
+            src_ref=parts.at[other, pl.ds(first, count)],
             dst_ref=moved.at[other, pl.ds(first, count)],
             send_sem=a_send.at[other, chunk], recv_sem=a_recv.at[other, chunk],
             device_id={"pair": other},
@@ -236,8 +218,55 @@
             device_id={"fold": block * 2 + half},
         )
 
-    def own_parts():
-        return pltpu.make_async_copy(parts_ref.at[pair], moved.at[pair], copy_sem)
+    def own_parts(chunk):
+        first, count = slabs_of[chunk]
+        return pltpu.make_async_copy(
+            parts.at[pair, pl.ds(first, count)], moved.at[pair, pl.ds(first, count)], copy_sem
+        )
+
+    def pack_t(chunk):
+        first, count = taken[chunk]
+
+        def one(step, carry):
+            target = turn(step)
+            load_t(step, chunk).wait()
+            slot = step % 2
+            own_rows = narrow(
+                label_of(fold * a_rows + target % split * rows + column(rows), vir_ends)
+            )
+            i_label = label_of(window_i[target // split], occ_ends)
+            tails = []
+            for k in range(first, first + count):
+                lanes = narrow(vir_line ^ occ_wide[pair * k_local + k] ^ i_label)
+                chosen = fold_columns(raw_t[slot, k - first], own_rows, lanes)
+                base = k // group * (group + 1)
+                parts[target, base + k % group] = chosen[:, :LANES]
+                tails.append(chosen[:, LANES:])
+                if k == k_local - 1:
+                    tails += [jnp.zeros_like(tails[0])] * (group - len(tails))
+                if len(tails) == group:
+                    parts[target, base + group] = jnp.concatenate(tails, axis=1)
+                    tails = []
+
+            @pl.when(step < n_pair - 1)
+            def _():
+                to_pair(step, chunk).start()
+
+            @pl.when(step + 2 < n_pair)
+            def _():
+                load_t(step + 2, chunk).start()
+
+            if chunk + 1 < chunks and taken[chunk + 1] is not None:
+
+                @pl.when(step + 2 >= n_pair)
+                def _():
+                    load_t(step + 2 - n_pair, chunk + 1).start()
+
+            return carry
+
+        lax.fori_loop(0, n_pair, one, 0)
+        own_parts(chunk).start()
+        own_parts(chunk).wait()
 
     loads = raw_w.shape[2]
     n_loads = occ_total // loads
@@ -252,9 +281,9 @@
         load_w(step).wait()
         slot = step % 2
         for k in range(loads):
-            lanes = narrow(line_ref[...] ^ label_ref[step * loads + k])
+            lanes = narrow(vir_line ^ occ_wide[step * loads + k])
             values = raw_w[slot, :, k].reshape(c_local * j_local, vir_total)
-            chosen = fold_columns(values, cj_ref[...], lanes).astype(jnp.float32)
+            chosen = fold_columns(values, narrow(cj_ref[...]), lanes).astype(jnp.float32)
             main_w[...] = chosen[:, :LANES]
             rest_w[:, :rest] = chosen[:, LANES:]
             block = step * (loads // 4) + k // 4
@@ -296,12 +325,14 @@
         first, count = spans[chunk]
         start, width = lanes_of[chunk]
         if slabs_of[chunk] is not None:
-            for step in range(1, n_pair):
+            for step in range(n_pair - 1):
                 from_pair(step, chunk).wait_recv()
+        own_rows = label_of(fold * a_rows + pair % split * rows + column(rows), vir_ends)
+        own_rows = own_rows ^ label_of(window_i[pair // split], occ_ends)
 
         def quarter(step, carry):
             q = flip(fold // here, step, FOLDS)
-            labels = narrow(own_ref[...] ^ vir_ref[q])
+            labels = narrow(own_rows ^ label_of(q * v_pack + line(v_pack), vir_ends))
             pieces = [[] for _ in range(here)]
             for kappa in range(first, first + count):
                 chosen = jnp.zeros((rows, v_pack), moved.dtype)
@@ -313,7 +344,7 @@
                         [moved[side, base + inner % group], moved[side, base + group][:, tail:tail + rest]],
                         axis=1,
                     )
-                    chosen = jnp.where(labels == occ_ref[k], piece, chosen)
+                    chosen = jnp.where(labels == occ_short[k], piece, chosen)
                 for f in range(here):
                     pieces[f].append(chosen[:, f * c_local:(f + 1) * c_local])
             spare = width - count * c_local
@@ -345,7 +376,8 @@
         for other in range(n_y):
             from_core(source, other, chunk).wait_recv()
         left = jnp.concatenate([held[source, p, :, start:start + depth] for p in range(n_pair)], axis=0)
-        labels = row_ref[source]
+        own_rows = label_of(source * a_rows + column(a_rows), vir_ends)
+        labels = narrow(jnp.concatenate([own_rows ^ i_label for i_label in i_labels], axis=0))
         sums = [None] * j_local
         if chunk:
             sums = [total[source, j] for j in range(j_local)]
@@ -375,21 +407,37 @@
             @pl.when(step == 1)
             def _():
                 for j in range(j_local):
-                    out_ref[j] = near[j]
+                    kept[j] = near[j]
 
             @pl.when(step > 1)
             def _():
                 encode(near, z_out.at[block])
                 over_z(block, outer).start()
 
-    for chunk in range(chunks):
-        if slabs_of[chunk] is not None:
-            for step in range(1, n_pair):
-                to_pair(step, chunk).start()
-    own_parts().start()
+    load_t(0, 0).start()
+    load_t(1, 0).start()
     load_w(0).start()
     load_w(1).start()
-    own_parts().wait()
+    places = lax.broadcasted_iota(jnp.int32, (occ_total, 1, vir_total), 0)
+    occ_wide[...] = label_of(places, occ_ends)
+    occ_short[...] = narrow(label_of(places[:, :, :v_pack], occ_ends))
+    c_of, j_of = split_by(column(c_local * j_local), j_local)
+    j_mixed = functools.reduce(jnp.add, [jnp.where(j_of == j, j_labels[j], 0) for j in range(j_local)])
+    cj_ref[...] = label_of(fold * c_local + c_of, vir_ends) ^ j_mixed
+    kappa_of, c_of = split_by(line(k_pack * c_local), c_local)
+    c_mixed = label_of(fold * c_local + c_of, vir_ends)
+    for s in range(FOLDS):
+        col_ref[s] = narrow(label_of(s * k_pack + kappa_of, occ_ends) ^ c_mixed)
+    barrier = pltpu.get_barrier_semaphore()
+    for step in range(1, n_fold):
+        pl.semaphore_signal(barrier, device_id={"fold": (fold + step) % n_fold})
+    for step in range(1, n_pair):
+        pl.semaphore_signal(barrier, device_id={"pair": (pair + step) % n_pair})
+    pl.semaphore_wait(barrier, n_fold + n_pair - 2)
+
+    for chunk in range(chunks):
+        if taken[chunk] is not None:
+            pack_t(chunk)
     lax.fori_loop(0, n_loads // 2, pack_w, 0)
     pack_k(0)
     lax.fori_loop(n_loads // 2, n_loads, pack_w, 0)
@@ -430,14 +478,28 @@
         over_z(block, block).wait_recv()
         far = decode(z_in[block], j_local, v_pack)
         for j in range(j_local):
-            out_ref[j] += far[j]
+            kept[j] += far[j]
         return carry
 
     lax.fori_loop(1, n_outer, finish, 0)
+
+    for i in range(n_i):
+        for j in range(j_local):
+            own = pl.ds(j, a_rows, stride=j_local)
+            values = kept[j, i * a_rows:(i + 1) * a_rows]
+            main_w[own, :] = values[:, :LANES]
+            rest_w[own, :rest] = values[:, LANES:]
+        values = jnp.concatenate([main_w[...], rest_w[:, :rest]], axis=1)
+        labels = cj_ref[...] ^ i_labels[i]
+        full = [
+            jnp.where(labels == vir_line[:, q * v_pack:(q + 1) * v_pack], values, 0.0) for q in range(FOLDS)
+        ]
+        full = jnp.concatenate(full, axis=1).astype(out_ref.dtype)
+        out_ref[i] = full.reshape(a_rows, j_local, vir_total)
 
     for chunk in range(chunks):
         if slabs_of[chunk] is not None:
-            for step in range(1, n_pair):
+            for step in range(n_pair - 1):
                 to_pair(step, chunk).wait_send()
 
         def drain(source, carry):
@@ -465,30 +527,40 @@
     lax.fori_loop(0, n_outer, drain_sums, 0)
 
 
-def contract_all(
-    n_pair, n_fold, parts, cycle_block, occ_labels, own_labels, vir_labels, cj_labels, row_labels, col_labels
-):
-    _, slabs, rows, _ = parts.shape
+def body(n_pair, n_fold, amplitudes, cycle_block, occ_sizes, vir_sizes, window_i, window_occ):
     c_local, occ_total, j_local, vir_total = cycle_block.shape
+    n_i, k_local, a_rows, _ = amplitudes.shape
     v_pack = vir_total // FOLDS
-    depth = col_labels.shape[-1]
+    split = n_pair // n_i
+    rows = a_rows // split
+    group = LANES // (v_pack - LANES)
+    slabs = -(-k_local // group) * (group + 1)
+    depth = occ_total // FOLDS * c_local
     wide = -(-depth // LANES) * LANES
     n_y, n_outer = n_pair // 2, n_fold // 2
     count = n_pair * rows
     lanes = (j_local + -(-(j_local * (v_pack - LANES) + 1) // LANES)) * LANES
-    chunks = len(spans_of(occ_total // FOLDS, c_local))
+    spans = spans_of(occ_total // FOLDS, c_local)
+    chunks = len(spans)
+    most = max(span[1] for span in spans) if k_local * FOLDS == occ_total else k_local
     loads = 8
-    occ = jnp.broadcast_to(narrow(occ_labels)[:, None, None], (occ_total, 1, v_pack))
     sems = pltpu.SemaphoreType.DMA
-    vmem = pl.BlockSpec(memory_space=pltpu.VMEM)
-    kind = parts.dtype
+    smem = pl.BlockSpec(memory_space=pltpu.SMEM)
+    hbm = pl.BlockSpec(memory_space=pl.ANY)
+    kind = amplitudes.dtype
     return pl.pallas_call(
         functools.partial(cycle_kernel, n_pair, n_fold),
-        out_shape=jax.ShapeDtypeStruct((j_local, count, v_pack), jnp.float32),
-        in_specs=[pl.BlockSpec(memory_space=pltpu.SMEM)] + [vmem] * 8 + [pl.BlockSpec(memory_space=pl.ANY)],
-        out_specs=vmem,
+        out_shape=jax.ShapeDtypeStruct((n_i, a_rows, j_local, vir_total), kind),
+        in_specs=[smem] * 4 + [hbm] * 2,
+        out_specs=pl.BlockSpec(memory_space=pltpu.VMEM),
         scratch_shapes=[
-            pltpu.VMEM(parts.shape, kind),
+            pltpu.VMEM((occ_total, 1, vir_total), jnp.int32),
+            pltpu.VMEM((occ_total, 1, v_pack), kind),
+            pltpu.VMEM((FOLDS, 1, depth), kind),
+            pltpu.VMEM((c_local * j_local, 1), jnp.int32),
+            pltpu.VMEM((n_pair, slabs, rows, LANES), kind),
+            pltpu.VMEM((2, most, rows, vir_total), kind),
+            pltpu.VMEM((n_pair, slabs, rows, LANES), kind),
             pltpu.VMEM((n_fold, rows, wide), kind),
             pltpu.VMEM((n_fold, n_pair, rows, wide), kind),
             pltpu.VMEM((j_local, occ_total // 4, 4 * c_local, v_pack), kind),
@@ -496,54 +568,23 @@
             pltpu.VMEM((c_local * j_local, LANES), jnp.float32),
             pltpu.VMEM((c_local * j_local, LANES), jnp.float32),
             pltpu.VMEM((n_fold, j_local, count, v_pack), jnp.float32),
+            pltpu.VMEM((j_local, count, v_pack), jnp.float32),
         ]
         + [pltpu.VMEM((n_outer, count, lanes), jnp.int16)] * 4
         + [
-            sems, sems((2,)), sems((n_pair, chunks)), sems((n_pair, chunks)),
+            sems, sems((2,)), sems((2,)), sems((n_pair, chunks)), sems((n_pair, chunks)),
             sems((n_fold, chunks)), sems((n_fold, chunks)),
             sems((n_fold, n_y, chunks)), sems((n_fold, n_y, chunks)),
             sems((n_fold, n_y, chunks)), sems((n_fold, n_y, chunks)),
             sems((n_outer,)), sems((n_outer,)), sems((n_outer,)), sems((n_outer,)),
         ],
         compiler_params=pltpu.CompilerParams(
-            collective_id=0, has_side_effects=True, vmem_limit_bytes=56 << 20
+            collective_id=0, has_side_effects=True, vmem_limit_bytes=60 << 20
         ),
     )(
-        occ_labels, occ, own_labels[:, None], vir_labels.reshape(FOLDS, 1, v_pack), vir_labels[None, :],
-        narrow(cj_labels).reshape(-1, 1), narrow(row_labels), narrow(col_labels), parts, cycle_block,
+        occ_sizes, vir_sizes, window_i, window_occ,
+        amplitudes.reshape(n_i, k_local, split, rows, vir_total), cycle_block,
     )
-
-
-def body(n_pair, n_fold, amplitudes, cycle_block, occ_sizes, vir_sizes, window_i, window_occ):
-    c_local, occ_total, j_local, vir_total = cycle_block.shape
-    n_i, k_local, a_rows, _ = amplitudes.shape
-    v_pack = vir_total // FOLDS
-    k_pack = occ_total // FOLDS
-    rows = n_i * a_rows // n_pair
-    fold = lax.axis_index("fold")
-    pair = lax.axis_index("pair")
-    occ_labels = irrep_labels(occ_sizes, occ_total)
-    vir_labels = irrep_labels(vir_sizes, vir_total)
-    c_labels = lax.dynamic_slice_in_dim(vir_labels, fold * c_local, c_local)
-    a_labels = lax.dynamic_slice_in_dim(vir_labels, fold * a_rows, a_rows)
-    k_labels = lax.dynamic_slice_in_dim(occ_labels, pair * k_local, k_local)
-    i_labels = label_lookup(window_i, occ_labels, occ_total)
-    j_orbitals = lax.dynamic_slice_in_dim(window_occ, pair * j_local, j_local)
-    j_labels = label_lookup(j_orbitals, occ_labels, occ_total)
-
-    parts = pack_t(amplitudes, i_labels[:, None] ^ k_labels[None, :], a_labels, vir_labels, n_pair)
-    ia_labels = (i_labels[:, None] ^ a_labels[None, :]).reshape(n_pair, rows)
-    own_labels = lax.dynamic_slice_in_dim(ia_labels, pair, 1)[0]
-    row_labels = (vir_labels.reshape(n_fold, 1, a_rows) ^ i_labels[None, :, None]).reshape(n_fold, -1, 1)
-    col_labels = (occ_labels[:, None] ^ c_labels[None, :]).reshape(FOLDS, 1, k_pack * c_local)
-    summed = contract_all(
-        n_pair, n_fold, parts, cycle_block, occ_labels, own_labels, vir_labels,
-        c_labels[:, None] ^ j_labels[None, :], row_labels, col_labels,
-    )
-    own = summed.astype(jnp.bfloat16).reshape(j_local, n_i, a_rows, v_pack).transpose(1, 2, 0, 3)
-    iaj = i_labels[:, None, None] ^ a_labels[None, :, None] ^ j_labels[None, None, :]
-    keep = iaj[..., None] == vir_labels
-    return jnp.where(keep, jnp.concatenate([own] * FOLDS, axis=-1), 0)
 
 
 def solution(mesh):

time: 138 us -> 120 us (0.87)
  other arithmetic: 10.5 us -> 0 us
  local copies, waits for them, and re-layouts: 10.2 us -> 2.6 us
    select_n x1 -> x0, other arithmetic: 4.46 us -> none  [body(): return jnp.where(keep, jnp.concatenate([own] * FOLDS, axis=-1), 0)]
    convert_element_type x5 -> x0, other arithmetic: 2.87 us -> none  [the longest x4 1.75 us: narrow(): return labels.astype(jnp.float32).astype(jnp.bfloat16)]
    unnamed x8 -> x1, local copies, waits for them, and re-layouts: 4.64 us -> 2.6 us
    another operation x2 -> x0, other arithmetic: 1.66 us -> none
    pallas_call x2 -> x1, Pallas kernels: 115 us -> 116 us  [body(): pl.pallas_call(functools.partial(cycle_kernel, n_pair, n_fold), out_shape...]
where the time goes in v3:
time: 120 us; the launch traced here: 119 us
  Pallas kernels  116 us (97%)
  local copies, waits for them, and re-layouts  2.6 us (2%)
    pallas_call x1, Pallas kernels, body(): pl.pallas_call(functools.partial(cycle_kernel, n_pair, n_fold), out_shape...  116 us
    unnamed x1, local copies, waits for them, and re-layouts  2.6 us

profile of v3, /device:TPU:17, one launch (start us, length us, event | category | flops | bytes accessed | tf_op | source)
XLA Modules:
  0.0 118.8 jit_solution(15680750547860447841)
XLA Ops:
  0.0 116.2 %shard_map.64 = bf16[4,80,2,640]{3,2,1,0:T(2,128)(2,1)} custom-call(s32[8]{0:T(128)} %occ_sizes.1, s32[8]{0:T(128)} %vir_sizes.1, s32[4]{0:T(128)} %window_i.1, s32[8]{0:T(128)} %window_occ.1, bf16[4,20,1,80,640]{4,3,2,1,0:T(8,128)(2,1)} %bitcast.1, bf16[80,80,2,640]{3,2,1,0:T(2,128)(2,1)} %w_hbm.1), custom_call_target="tpu_custom_call" | custom-call | tf_op jit(solution)/shard_map/pallas_call | solution.py:551
  116.2 2.6 %copy.8 = bf16[4,80,2,640]{3,2,1,0:T(2,128)(2,1)} copy(bf16[4,80,2,640]{3,2,1,0:T(2,128)(2,1)} %shard_map.64) | data formatting | bytes 1638400

commit v4 on v3

--- a/solution.py
+++ b/solution.py
@@ -10,7 +10,10 @@
 
 LANES = 128
 FOLDS = 4
+EARLY = 2
+READY = 6
 AHEAD = 3
+NEXT = 1
 STEPS = 32000.0
 FINE = 8.0
 
@@ -98,10 +101,10 @@
 
 def cycle_kernel(
     n_pair, n_fold, occ_sizes, vir_sizes, window_i, window_occ, t_hbm, w_hbm, out_ref,
-    occ_wide, occ_short, col_ref, cj_ref, parts, raw_t, moved, wide, held, packed_w, raw_w, main_w, rest_w,
-    total, kept, x_out, x_in, z_out, z_in,
+    occ_wide, col_ref, cj_ref, parts, raw_t, moved, wide, held, packed_w, raw_w, main_w, rest_w,
+    total, kept, x_out, x_in, z_out, z_in, m_in,
     copy_sem, t_sem, w_sem, a_send, a_recv, f_send, f_recv, y_send, y_recv, c_send, c_recv,
-    x_send, x_recv, z_send, z_recv,
+    x_send, x_recv, z_send, z_recv, m_recv,
 ):
     pair, fold = lax.axis_index("pair"), lax.axis_index("fold")
     n_y, n_outer, here = n_pair // 2, n_fold // 2, n_fold // FOLDS
@@ -218,6 +221,13 @@
             device_id={"fold": block * 2 + half},
         )
 
+    def to_near(block):
+        return pltpu.make_async_remote_copy(
+            src_ref=z_out.at[block], dst_ref=m_in.at[block],
+            send_sem=z_send.at[block], recv_sem=m_recv.at[block],
+            device_id={"fold": flip(outer, 1, n_outer) * 2 + half},
+        )
+
     def own_parts(chunk):
         first, count = slabs_of[chunk]
         return pltpu.make_async_copy(
@@ -237,7 +247,7 @@
             i_label = label_of(window_i[target // split], occ_ends)
             tails = []
             for k in range(first, first + count):
-                lanes = narrow(vir_line ^ occ_wide[pair * k_local + k] ^ i_label)
+                lanes = narrow(vir_line ^ occ_wide[pl.ds(pair * k_local + k, 1), :] ^ i_label)
                 chosen = fold_columns(raw_t[slot, k - first], own_rows, lanes)
                 base = k // group * (group + 1)
                 parts[target, base + k % group] = chosen[:, :LANES]
@@ -281,7 +291,7 @@
         load_w(step).wait()
         slot = step % 2
         for k in range(loads):
-            lanes = narrow(vir_line ^ occ_wide[step * loads + k])
+            lanes = narrow(vir_line ^ occ_wide[pl.ds(step * loads + k, 1), :])
             values = raw_w[slot, :, k].reshape(c_local * j_local, vir_total)
             chosen = fold_columns(values, narrow(cj_ref[...]), lanes).astype(jnp.float32)
             main_w[...] = chosen[:, :LANES]
@@ -299,8 +309,11 @@
 
         return carry
 
-    def source_of(step):
-        return flip(outer, step // 2, n_outer) * 2 + (half + 1 + step) % 2
+    def block_of(step, chunk):
+        return flip(outer, (step // 2 + (chunk == chunks - 1)) % n_outer, n_outer)
+
+    def source_of(step, chunk):
+        return block_of(step, chunk) * 2 + (half + 1 + step) % 2
 
     def relay(source, chunk):
         for step in range(1, n_y):
@@ -308,15 +321,16 @@
         over_core(source, 0, chunk).start()
 
     def fetch(step, chunk):
-        source = source_of(step)
-
-        @pl.when(step != 1)
+        source = source_of(step, chunk)
+
+        @pl.when(source != fold)
         def _():
             from_fold(source, chunk).wait_recv()
             relay(source, chunk)
 
+
     def pass_on(step, chunk):
-        source = source_of(step)
+        source = source_of(step, chunk)
         for other in range(1, n_y):
             from_y(source, other, chunk).wait_recv()
             over_core(source, other, chunk).start()
@@ -344,7 +358,7 @@
                         [moved[side, base + inner % group], moved[side, base + group][:, tail:tail + rest]],
                         axis=1,
                     )
-                    chosen = jnp.where(labels == occ_short[k], piece, chosen)
+                    chosen = jnp.where(labels == narrow(occ_wide[k:k + 1, :v_pack]), piece, chosen)
                 for f in range(here):
                     pieces[f].append(chosen[:, f * c_local:(f + 1) * c_local])
             spare = width - count * c_local
@@ -369,8 +383,8 @@
         relay(fold, chunk)
 
     def multiply(step, chunk):
-        source = source_of(step)
-        block = flip(outer, step // 2, n_outer)
+        source = source_of(step, chunk)
+        block = block_of(step, chunk)
         first, count = spans[chunk]
         start, depth = first * c_local, count * c_local
         for other in range(n_y):
@@ -398,29 +412,53 @@
             encode([total[source, j] for j in range(j_local)], x_out.at[block])
             over_x(block).start()
 
-        @pl.when(step % 2 == 1)
-        def _():
-            over_x(block).wait_recv()
-            near = decode(x_in[block], j_local, v_pack)
-            near = [total[source, j] + near[j] for j in range(j_local)]
-
-            @pl.when(step == 1)
-            def _():
-                for j in range(j_local):
-                    kept[j] = near[j]
-
-            @pl.when(step > 1)
-            def _():
-                encode(near, z_out.at[block])
-                over_z(block, outer).start()
+        @pl.when((step % 2 == 1) & (step > 1))
+        def _():
+            settle(step // 2)
+
+    def settle(turned):
+        block = flip(outer, turned, n_outer)
+        over_x(block).wait_recv()
+        near = decode(x_in[block], j_local, v_pack)
+        near = [total[block * 2 + half, j] + near[j] for j in range(j_local)]
+        late = 0 if isinstance(turned, int) else 1
+        for j in range(j_local):
+            kept[late, j] = near[j]
+
+        @pl.when((turned % 2 == 1) & (turned > 1))
+        def _():
+            to_near(block).wait_recv()
+            more = decode(m_in[block], j_local, v_pack)
+            for j in range(j_local):
+                kept[1, j] += more[j]
+
+        @pl.when(turned > 0)
+        def _():
+            encode([kept[1, j] for j in range(j_local)], z_out.at[block])
+
+        @pl.when((turned % 2 == 0) & (turned > 0))
+        def _():
+            to_near(block).start()
+
+        @pl.when(turned % 2 == 1)
+        def _():
+            over_z(block, outer).start()
 
     load_t(0, 0).start()
     load_t(1, 0).start()
     load_w(0).start()
     load_w(1).start()
-    places = lax.broadcasted_iota(jnp.int32, (occ_total, 1, vir_total), 0)
-    occ_wide[...] = label_of(places, occ_ends)
-    occ_short[...] = narrow(label_of(places[:, :, :v_pack], occ_ends))
+    barrier = pltpu.get_barrier_semaphore()
+    for step in range(1, n_fold):
+        pl.semaphore_signal(barrier, device_id={"fold": (fold + step) % n_fold})
+    for step in range(1, n_pair):
+        pl.semaphore_signal(barrier, device_id={"pair": (pair + step) % n_pair})
+
+    occ_wide[...] = label_of(lax.broadcasted_iota(jnp.int32, (occ_total, vir_total), 0), occ_ends)
+    pl.semaphore_wait(barrier, n_fold + n_pair - 2)
+    for chunk in range(chunks):
+        if taken[chunk] is not None:
+            pack_t(chunk)
     c_of, j_of = split_by(column(c_local * j_local), j_local)
     j_mixed = functools.reduce(jnp.add, [jnp.where(j_of == j, j_labels[j], 0) for j in range(j_local)])
     cj_ref[...] = label_of(fold * c_local + c_of, vir_ends) ^ j_mixed
@@ -428,35 +466,38 @@
     c_mixed = label_of(fold * c_local + c_of, vir_ends)
     for s in range(FOLDS):
         col_ref[s] = narrow(label_of(s * k_pack + kappa_of, occ_ends) ^ c_mixed)
-    barrier = pltpu.get_barrier_semaphore()
-    for step in range(1, n_fold):
-        pl.semaphore_signal(barrier, device_id={"fold": (fold + step) % n_fold})
-    for step in range(1, n_pair):
-        pl.semaphore_signal(barrier, device_id={"pair": (pair + step) % n_pair})
-    pl.semaphore_wait(barrier, n_fold + n_pair - 2)
-
-    for chunk in range(chunks):
-        if taken[chunk] is not None:
-            pack_t(chunk)
-    lax.fori_loop(0, n_loads // 2, pack_w, 0)
+    lax.fori_loop(0, EARLY, pack_w, 0)
     pack_k(0)
-    lax.fori_loop(n_loads // 2, n_loads, pack_w, 0)
+
+    def pack_w_relaying(step, carry):
+        pack_w(step, carry)
+
+        @pl.when((step > EARLY) & (step <= EARLY + READY))
+        def _():
+            fetch(step - EARLY - 1, 0)
+
+        return carry
+
+    lax.fori_loop(EARLY, n_loads, pack_w_relaying, 0)
     for chunk in range(1, chunks):
         pack_k(chunk)
 
-    for step in range(AHEAD):
+    for step in range(READY, n_fold):
         fetch(step, 0)
-    pass_on(0, 0)
+    for step in range(NEXT):
+        pass_on(step, 0)
     for chunk in range(chunks):
 
         def source_step(step, carry):
-            @pl.when(step + AHEAD < n_fold)
+            if chunk:
+
+                @pl.when(step + AHEAD < n_fold)
+                def _():
+                    fetch(step + AHEAD, chunk)
+
+            @pl.when(step + NEXT < n_fold)
             def _():
-                fetch(step + AHEAD, chunk)
-
-            @pl.when(step + 1 < n_fold)
-            def _():
-                pass_on(step + 1, chunk)
+                pass_on(step + NEXT, chunk)
 
             if chunk < chunks - 1:
 
@@ -464,29 +505,31 @@
                 def _():
                     fetch(step + AHEAD - n_fold, chunk + 1)
 
-                @pl.when(step + 1 >= n_fold)
+                @pl.when(step + NEXT >= n_fold)
                 def _():
-                    pass_on(step + 1 - n_fold, chunk + 1)
+                    pass_on(step + NEXT - n_fold, chunk + 1)
 
             multiply(step, chunk)
             return carry
 
         lax.fori_loop(0, n_fold, source_step, 0)
 
+    settle(0)
+
     def finish(step, carry):
-        block = flip(outer, step, n_outer)
+        block = flip(outer, step * 2 + 1, n_outer)
         over_z(block, block).wait_recv()
         far = decode(z_in[block], j_local, v_pack)
         for j in range(j_local):
-            kept[j] += far[j]
+            kept[0, j] += far[j]
         return carry
 
-    lax.fori_loop(1, n_outer, finish, 0)
+    lax.fori_loop(0, n_outer // 2, finish, 0)
 
     for i in range(n_i):
         for j in range(j_local):
             own = pl.ds(j, a_rows, stride=j_local)
-            values = kept[j, i * a_rows:(i + 1) * a_rows]
+            values = kept[0, j, i * a_rows:(i + 1) * a_rows]
             main_w[own, :] = values[:, :LANES]
             rest_w[own, :rest] = values[:, LANES:]
         values = jnp.concatenate([main_w[...], rest_w[:, :rest]], axis=1)
@@ -554,8 +597,7 @@
         in_specs=[smem] * 4 + [hbm] * 2,
         out_specs=pl.BlockSpec(memory_space=pltpu.VMEM),
         scratch_shapes=[
-            pltpu.VMEM((occ_total, 1, vir_total), jnp.int32),
-            pltpu.VMEM((occ_total, 1, v_pack), kind),
+            pltpu.VMEM((occ_total, vir_total), jnp.int32),
             pltpu.VMEM((FOLDS, 1, depth), kind),
             pltpu.VMEM((c_local * j_local, 1), jnp.int32),
             pltpu.VMEM((n_pair, slabs, rows, LANES), kind),
@@ -568,15 +610,15 @@
             pltpu.VMEM((c_local * j_local, LANES), jnp.float32),
             pltpu.VMEM((c_local * j_local, LANES), jnp.float32),
             pltpu.VMEM((n_fold, j_local, count, v_pack), jnp.float32),
-            pltpu.VMEM((j_local, count, v_pack), jnp.float32),
+            pltpu.VMEM((2, j_local, count, v_pack), jnp.float32),
         ]
-        + [pltpu.VMEM((n_outer, count, lanes), jnp.int16)] * 4
+        + [pltpu.VMEM((n_outer, count, lanes), jnp.int16)] * 5
         + [
             sems, sems((2,)), sems((2,)), sems((n_pair, chunks)), sems((n_pair, chunks)),
             sems((n_fold, chunks)), sems((n_fold, chunks)),
             sems((n_fold, n_y, chunks)), sems((n_fold, n_y, chunks)),
             sems((n_fold, n_y, chunks)), sems((n_fold, n_y, chunks)),
-            sems((n_outer,)), sems((n_outer,)), sems((n_outer,)), sems((n_outer,)),
+            sems((n_outer,)), sems((n_outer,)), sems((n_outer,)), sems((n_outer,)), sems((n_outer,)),
         ],
         compiler_params=pltpu.CompilerParams(
             collective_id=0, has_side_effects=True, vmem_limit_bytes=60 << 20

time: 120 us -> 108 us (0.900)
  Pallas kernels: 116 us -> 104 us
    pallas_call x1, Pallas kernels: 116 us -> 104 us  [body(): pl.pallas_call(functools.partial(cycle_kernel, n_pair, n_fold), out_shape...]
where the time goes in v4:
time: 108 us; the launch traced here: 107 us
  Pallas kernels  104 us (96%)
  local copies, waits for them, and re-layouts  2.6 us (2%)
    pallas_call x1, Pallas kernels, body(): pl.pallas_call(functools.partial(cycle_kernel, n_pair, n_fold), out_shape...  104 us
    unnamed x1, local copies, waits for them, and re-layouts  2.6 us

profile of v4, /device:TPU:17, one launch (start us, length us, event | category | flops | bytes accessed | tf_op | source)
XLA Modules:
  0.0 106.7 jit_solution(8162287525834284704)
XLA Ops:
  0.0 104.1 %shard_map.64 = bf16[4,80,2,640]{3,2,1,0:T(2,128)(2,1)} custom-call(s32[8]{0:T(128)} %occ_sizes.1, s32[8]{0:T(128)} %vir_sizes.1, s32[4]{0:T(128)} %window_i.1, s32[8]{0:T(128)} %window_occ.1, bf16[4,20,1,80,640]{4,3,2,1,0:T(8,128)(2,1)} %bitcast.1, bf16[80,80,2,640]{3,2,1,0:T(2,128)(2,1)} %w_hbm.1), custom_call_target="tpu_custom_call" | custom-call | tf_op jit(solution)/shard_map/pallas_call | solution.py:594
  104.1 2.6 %copy.8 = bf16[4,80,2,640]{3,2,1,0:T(2,128)(2,1)} copy(bf16[4,80,2,640]{3,2,1,0:T(2,128)(2,1)} %shard_map.64) | data formatting | bytes 1638400

commit v5 on v4

--- a/solution.py
+++ b/solution.py
@@ -10,7 +10,8 @@
 
 LANES = 128
 FOLDS = 4
-EARLY = 2
+EARLY = 1
+LATE = 6
 READY = 6
 AHEAD = 3
 NEXT = 1
@@ -323,7 +324,7 @@
     def fetch(step, chunk):
         source = source_of(step, chunk)
 
-        @pl.when(source != fold)
+        @pl.when((source != fold) if chunk == 0 else (source // 2 != outer))
         def _():
             from_fold(source, chunk).wait_recv()
             relay(source, chunk)
@@ -478,12 +479,17 @@
 
         return carry
 
-    lax.fori_loop(EARLY, n_loads, pack_w_relaying, 0)
+    lax.fori_loop(EARLY, LATE, pack_w_relaying, 0)
     for chunk in range(1, chunks):
         pack_k(chunk)
+    lax.fori_loop(LATE, n_loads, pack_w_relaying, 0)
 
     for step in range(READY, n_fold):
         fetch(step, 0)
+    for chunk in range(1, chunks):
+        beside = outer * 2 + 1 - half
+        from_fold(beside, chunk).wait_recv()
+        relay(beside, chunk)
     for step in range(NEXT):
         pass_on(step, 0)
     for chunk in range(chunks):

time: 108 us -> 104 us (0.963)
  Pallas kernels: 104 us -> 101 us
    pallas_call x1, Pallas kernels: 104 us -> 101 us  [body(): pl.pallas_call(functools.partial(cycle_kernel, n_pair, n_fold), out_shape...]
where the time goes in v5:
time: 104 us; the launch traced here: 103 us
  Pallas kernels  101 us (97%)
  local copies, waits for them, and re-layouts  2.6 us (2%)
    pallas_call x1, Pallas kernels, body(): pl.pallas_call(functools.partial(cycle_kernel, n_pair, n_fold), out_shape...  101 us
    unnamed x1, local copies, waits for them, and re-layouts  2.6 us

profile of v5, /device:TPU:17, one launch (start us, length us, event | category | flops | bytes accessed | tf_op | source)
XLA Modules:
  0.0 103.5 jit_solution(11049437121612144160)
XLA Ops:
  0.0 100.9 %shard_map.64 = bf16[4,80,2,640]{3,2,1,0:T(2,128)(2,1)} custom-call(s32[8]{0:T(128)} %occ_sizes.1, s32[8]{0:T(128)} %vir_sizes.1, s32[4]{0:T(128)} %window_i.1, s32[8]{0:T(128)} %window_occ.1, bf16[4,20,1,80,640]{4,3,2,1,0:T(8,128)(2,1)} %bitcast.1, bf16[80,80,2,640]{3,2,1,0:T(2,128)(2,1)} %w_hbm.1), custom_call_target="tpu_custom_call" | custom-call | tf_op jit(solution)/shard_map/pallas_call | solution.py:600
  100.9 2.6 %copy.8 = bf16[4,80,2,640]{3,2,1,0:T(2,128)(2,1)} copy(bf16[4,80,2,640]{3,2,1,0:T(2,128)(2,1)} %shard_map.64) | data formatting | bytes 1638400

commit v6 on v5

--- a/solution.py
+++ b/solution.py
@@ -388,6 +388,12 @@
         block = block_of(step, chunk)
         first, count = spans[chunk]
         start, depth = first * c_local, count * c_local
+        if chunk == chunks - 1:
+
+            @pl.when((step % 2 == 1) & (step > 1))
+            def _():
+                settle(step // 2)
+
         for other in range(n_y):
             from_core(source, other, chunk).wait_recv()
         left = jnp.concatenate([held[source, p, :, start:start + depth] for p in range(n_pair)], axis=0)
@@ -412,10 +418,6 @@
         def _():
             encode([total[source, j] for j in range(j_local)], x_out.at[block])
             over_x(block).start()
-
-        @pl.when((step % 2 == 1) & (step > 1))
-        def _():
-            settle(step // 2)
 
     def settle(turned):
         block = flip(outer, turned, n_outer)

time: 104 us -> 102 us (0.981)
  Pallas kernels: 101 us -> 98.8 us
    pallas_call x1, Pallas kernels: 101 us -> 98.8 us  [body(): pl.pallas_call(functools.partial(cycle_kernel, n_pair, n_fold), out_shape...]
where the time goes in v6:
time: 102 us; the launch traced here: 101 us
  Pallas kernels  98.8 us (97%)
  local copies, waits for them, and re-layouts  2.6 us (3%)
    pallas_call x1, Pallas kernels, body(): pl.pallas_call(functools.partial(cycle_kernel, n_pair, n_fold), out_shape...  98.8 us
    unnamed x1, local copies, waits for them, and re-layouts  2.6 us

profile of v6, /device:TPU:17, one launch (start us, length us, event | category | flops | bytes accessed | tf_op | source)
XLA Modules:
  0.0 101.4 jit_solution(14296944127421980093)
XLA Ops:
  0.0 98.8 %shard_map.64 = bf16[4,80,2,640]{3,2,1,0:T(2,128)(2,1)} custom-call(s32[8]{0:T(128)} %occ_sizes.1, s32[8]{0:T(128)} %vir_sizes.1, s32[4]{0:T(128)} %window_i.1, s32[8]{0:T(128)} %window_occ.1, bf16[4,20,1,80,640]{4,3,2,1,0:T(8,128)(2,1)} %bitcast.1, bf16[80,80,2,640]{3,2,1,0:T(2,128)(2,1)} %w_hbm.1), custom_call_target="tpu_custom_call" | custom-call | tf_op jit(solution)/shard_map/pallas_call | solution.py:602
  98.8 2.6 %copy.8 = bf16[4,80,2,640]{3,2,1,0:T(2,128)(2,1)} copy(bf16[4,80,2,640]{3,2,1,0:T(2,128)(2,1)} %shard_map.64) | data formatting | bytes 1638400

commit v7 on v6

--- a/solution.py
+++ b/solution.py
@@ -12,7 +12,7 @@
 FOLDS = 4
 EARLY = 1
 LATE = 6
-READY = 6
+READY = 8
 AHEAD = 3
 NEXT = 1
 STEPS = 32000.0

time: 102 us -> 102 us (level)
  no operation moved by 1% of the time
where the time goes in v7:
time: 102 us; the launch traced here: 101 us
  Pallas kernels  98.8 us (97%)
  local copies, waits for them, and re-layouts  2.6 us (3%)
    pallas_call x1, Pallas kernels, body(): pl.pallas_call(functools.partial(cycle_kernel, n_pair, n_fold), out_shape...  98.8 us
    unnamed x1, local copies, waits for them, and re-layouts  2.6 us

profile of v7, /device:TPU:17, one launch (start us, length us, event | category | flops | bytes accessed | tf_op | source)
XLA Modules:
  0.0 101.4 jit_solution(9549889934042275111)
XLA Ops:
  0.0 98.8 %shard_map.64 = bf16[4,80,2,640]{3,2,1,0:T(2,128)(2,1)} custom-call(s32[8]{0:T(128)} %occ_sizes.1, s32[8]{0:T(128)} %vir_sizes.1, s32[4]{0:T(128)} %window_i.1, s32[8]{0:T(128)} %window_occ.1, bf16[4,20,1,80,640]{4,3,2,1,0:T(8,128)(2,1)} %bitcast.1, bf16[80,80,2,640]{3,2,1,0:T(2,128)(2,1)} %w_hbm.1), custom_call_target="tpu_custom_call" | custom-call | tf_op jit(solution)/shard_map/pallas_call | solution.py:602
  98.8 2.6 %copy.8 = bf16[4,80,2,640]{3,2,1,0:T(2,128)(2,1)} copy(bf16[4,80,2,640]{3,2,1,0:T(2,128)(2,1)} %shard_map.64) | data formatting | bytes 1638400
